TPU v7x, 128 devices: a whole 4x4x4 slice. The times are simulated.
128 devices in a mesh: dom: 16 (over y, x), sub: 8 (over z, core).
Axes of the slice: x: 4, y: 4, z: 4, core: 2. Of those that a mesh axis runs over, the one named last changes fastest.
Arguments:
- old_coef: float32 [100, 524288], P(None, ('dom', 'sub')), may hold values from -6 to 6
- old_index: int32 [1048576], P(('dom', 'sub')), may hold values from 0 to 4095
- pair_count: int32 [128, 128], replicated, may hold values from 16 to 64, as said below
- new_index: int32 [1048576], P(('dom', 'sub')), may hold values from 0 to 2047
- old_points: float32 [3, 25165824], P(None, ('dom', 'sub')), may hold values from 0 to 1
- new_points: float32 [3, 25165824], P(None, ('dom', 'sub')), may hold values from 0 to 1
- weights: float32 [25165824], P(('dom', 'sub')), may hold values from 0.1 to 1
- jacobian: float32 [262144], P(('dom', 'sub')), may hold values from 0.5 to 2
- minv_ref: float32 [20, 20], replicated, may hold values from -0.06 to 2.5, as said below
- send_order: int32 [128, 2048], P(('dom', 'sub')), may hold values from 0 to 2047, each once within a row
Outputs:
- solver_coef: float32 [100, 262144], P(None, ('dom', 'sub'))
Inputs may be any that keep to these rules, and one draw needn't show every extreme that they name: `pair_count`: entry (s, d) is how many of the 64 slots from s to d are used, the first ones; each row has an entry equal to 64, and one column is 64 in every row. `minv_ref`: symmetric with a dominant diagonal. `send_order`: each row is a permutation.
All inputs are finite; a program needn't handle non-finite values.
Results may differ from a plain program's by a relative error of at most 0.0003.
Values sent between devices are 32-bit elements; how exact they have to be, the bound alone decides.
No kernel may reach another device: no remote copies, remote signals or barrier semaphores. Data moves between devices by JAX's collectives and lax.ppermute only.
A program may use at most 192 MiB of HBM per device.

v0:
```python
import math

import jax
import jax.numpy as jnp
from jax import lax
from jax.sharding import PartitionSpec as P

VARS = 5
MODES = 20


def modal_basis(points):
    first, second, third = (points[0], points[1], points[2])
    unit = jnp.ones_like(first)
    first_pow = [unit, first, first * first, first * first * first]
    second_pow = [unit, second, second * second, second * second * second]
    third_pow = [unit, third, third * third, third * third * third]
    rows = []
    for degree in range(4):
        for power_a in range(degree, -1, -1):
            for power_b in range(degree - power_a, -1, -1):
                rows.append(
                    first_pow[power_a] * second_pow[power_b] * third_pow[degree - power_a - power_b]
                )
    return rows


def select_columns(source, index, mask, block):
    total_rows, width = source.shape
    count = index.shape[0]
    iota_rows = jnp.arange(width, dtype=jnp.int32)

    def step(turn, result):
        start = turn * block
        wanted = lax.dynamic_slice_in_dim(index, start, block, 0)
        keep = lax.dynamic_slice_in_dim(mask, start, block, 0)
        onehot = ((iota_rows[:, None] == wanted[None, :]) & keep[None, :]).astype(jnp.float32)
        picked = jnp.dot(
            source, onehot, precision=lax.Precision.HIGHEST, preferred_element_type=jnp.float32
        )
        return lax.dynamic_update_slice_in_dim(result, picked, start, 1)

    result = jnp.zeros((total_rows, count), jnp.float32)
    return lax.fori_loop(0, count // block, step, result)


def local(
    old_coef,
    old_index,
    pair_count,
    new_index,
    old_points,
    new_points,
    weights,
    jacobian,
    minv_ref,
    send_order,
):
    devices = lax.axis_size(("dom", "sub"))
    myself = lax.axis_index(("dom", "sub"))
    total_rows = old_coef.shape[0]
    slot_count = old_index.shape[0]
    capacity = slot_count // devices
    new_count = jacobian.shape[0]
    quad_count = weights.shape[0] // slot_count
    slot_block = math.gcd(slot_count, 1024)
    new_block = math.gcd(new_count, 1024)
    counts = lax.dynamic_slice_in_dim(pair_count, myself, 1, 0)[0]
    live = (jnp.arange(capacity, dtype=jnp.int32)[None, :] < counts[:, None]).reshape(-1)
    outgoing = select_columns(old_coef, old_index, live, slot_block)
    incoming = lax.all_to_all(outgoing, ("dom", "sub"), split_axis=1, concat_axis=1, tiled=True)
    psi_old = modal_basis(old_points.reshape(3, quad_count, slot_count))
    psi_new = modal_basis(new_points.reshape(3, quad_count, slot_count))
    coefs = incoming.reshape(VARS, MODES, slot_count)
    values = coefs[:, 0, None, :] * psi_old[0][None]
    for mode in range(1, MODES):
        values = values + coefs[:, mode, None, :] * psi_old[mode][None]
    weighted = values * weights.reshape(quad_count, slot_count)[None]
    basis_new = jnp.stack(psi_new)
    moments = basis_new[None, :, 0, :] * weighted[:, None, 0, :]
    for point in range(1, quad_count):
        moments = moments + basis_new[None, :, point, :] * weighted[:, None, point, :]
    moments = moments.reshape(total_rows, slot_count)
    iota_new = jnp.arange(new_count, dtype=jnp.int32)

    def deposit(turn, total):
        start = turn * slot_block
        targets = lax.dynamic_slice_in_dim(new_index, start, slot_block, 0)
        part_moments = lax.dynamic_slice_in_dim(moments, start, slot_block, 1)
        onehot = (targets[:, None] == iota_new[None, :]).astype(jnp.float32)
        return total + jnp.dot(
            part_moments,
            onehot,
            precision=lax.Precision.HIGHEST,
            preferred_element_type=jnp.float32,
        )

    rhs = lax.fori_loop(
        0, slot_count // slot_block, deposit, jnp.zeros((total_rows, new_count), jnp.float32)
    )
    rhs_modes = rhs.reshape(VARS, MODES, new_count)
    projected = minv_ref[None, :, 0, None] * rhs_modes[:, 0, None, :]
    for mode in range(1, MODES):
        projected = projected + minv_ref[None, :, mode, None] * rhs_modes[:, mode, None, :]
    projected = (projected / jacobian[None, None, :]).reshape(total_rows, new_count)
    every = jnp.ones((new_count,), dtype=jnp.bool_)
    leaving = select_columns(projected, send_order[0], every, new_block)
    solver_coef = lax.all_to_all(leaving, ("dom", "sub"), split_axis=1, concat_axis=1, tiled=True)
    return solver_coef


def solution(mesh):
    placed = (
        P(None, ("dom", "sub")),
        P(("dom", "sub")),
        P(),
        P(("dom", "sub")),
        P(None, ("dom", "sub")),
        P(None, ("dom", "sub")),
        P(("dom", "sub")),
        P(("dom", "sub")),
        P(),
        P(("dom", "sub"), None),
    )
    return jax.shard_map(
        local, mesh=mesh, in_specs=placed, out_specs=P(None, ("dom", "sub")), check_vma=False
    )
```

profile of v0, /device:TPU:1, one launch (start us, length us, event | category | flops | bytes accessed | tf_op | source)
XLA Modules:
  0.0 564.0 jit_solution(12821667635861040523)
XLA Ops:
  1.4 67.2 %while.42 = (s32[]{:T(128)}, f32[100,8192]{1,0:T(8,128)S(1)}, s32[8192]{0:T(1024)}, pred[8192]{0:T(1024)(128)(4,1)S(1)}, f32[100,4096]{1,0:T(8,128)}, /*index=5*/s32[]{:T(128)}, s32[]{:T(128)}, s32[]{:T(128)}, s32[]{:T(128)}) while((s32[]{:T(128)}, f32[100,8192]{1,0:T(8,128)S(1)}, s32[8192]{0:T(1024)}, ...), condition=%wide.region_1.0_spmd.clone, body=%wide.region_0.0_spmd.clone.sunk | while | flops 5041553408 | bytes 2079895 | solution.py:44
  2.1 7.7 %fusion.114 = f32[100,8192]{1,0:T(8,128)S(1)} fusion(f32[100,8192]{1,0:T(8,128)S(1)} %get-tuple-element.1059, s32[]{:T(128)S(6)} %select_n.35, f32[100,4096]{1,0:T(8,128)} %get-tuple-element.1071, s32[1024]{0:T(1024)S(1)} %dynamic_slice.52, pred[1024]{0:T(1024)(128)(4,1)S(1)} %dynamic_slice.53), kind=kOutput, calls=%fused_computation.10.clone.1 | convolution fusion | flops 5041553408 | bytes 2069508 | tf_op jit(solution)/shard_map/while/body/eval_jaxpr/dot_general | solution.py:38
  10.5 7.7 %fusion.114 = f32[100,8192]{1,0:T(8,128)S(1)} fusion(f32[100,8192]{1,0:T(8,128)S(1)} %get-tuple-element.1059, s32[]{:T(128)S(6)} %select_n.35, f32[100,4096]{1,0:T(8,128)} %get-tuple-element.1071, s32[1024]{0:T(1024)S(1)} %dynamic_slice.52, pred[1024]{0:T(1024)(128)(4,1)S(1)} %dynamic_slice.53), kind=kOutput, calls=%fused_computation.10.clone.1 | convolution fusion | flops 5041553408 | bytes 2069508 | tf_op jit(solution)/shard_map/while/body/eval_jaxpr/dot_general | solution.py:38
  18.9 7.7 %fusion.114 = f32[100,8192]{1,0:T(8,128)S(1)} fusion(f32[100,8192]{1,0:T(8,128)S(1)} %get-tuple-element.1059, s32[]{:T(128)S(6)} %select_n.35, f32[100,4096]{1,0:T(8,128)} %get-tuple-element.1071, s32[1024]{0:T(1024)S(1)} %dynamic_slice.52, pred[1024]{0:T(1024)(128)(4,1)S(1)} %dynamic_slice.53), kind=kOutput, calls=%fused_computation.10.clone.1 | convolution fusion | flops 5041553408 | bytes 2069508 | tf_op jit(solution)/shard_map/while/body/eval_jaxpr/dot_general | solution.py:38
  27.3 7.7 %fusion.114 = f32[100,8192]{1,0:T(8,128)S(1)} fusion(f32[100,8192]{1,0:T(8,128)S(1)} %get-tuple-element.1059, s32[]{:T(128)S(6)} %select_n.35, f32[100,4096]{1,0:T(8,128)} %get-tuple-element.1071, s32[1024]{0:T(1024)S(1)} %dynamic_slice.52, pred[1024]{0:T(1024)(128)(4,1)S(1)} %dynamic_slice.53), kind=kOutput, calls=%fused_computation.10.clone.1 | convolution fusion | flops 5041553408 | bytes 2069508 | tf_op jit(solution)/shard_map/while/body/eval_jaxpr/dot_general | solution.py:38
  35.7 7.7 %fusion.114 = f32[100,8192]{1,0:T(8,128)S(1)} fusion(f32[100,8192]{1,0:T(8,128)S(1)} %get-tuple-element.1059, s32[]{:T(128)S(6)} %select_n.35, f32[100,4096]{1,0:T(8,128)} %get-tuple-element.1071, s32[1024]{0:T(1024)S(1)} %dynamic_slice.52, pred[1024]{0:T(1024)(128)(4,1)S(1)} %dynamic_slice.53), kind=kOutput, calls=%fused_computation.10.clone.1 | convolution fusion | flops 5041553408 | bytes 2069508 | tf_op jit(solution)/shard_map/while/body/eval_jaxpr/dot_general | solution.py:38
  44.1 7.7 %fusion.114 = f32[100,8192]{1,0:T(8,128)S(1)} fusion(f32[100,8192]{1,0:T(8,128)S(1)} %get-tuple-element.1059, s32[]{:T(128)S(6)} %select_n.35, f32[100,4096]{1,0:T(8,128)} %get-tuple-element.1071, s32[1024]{0:T(1024)S(1)} %dynamic_slice.52, pred[1024]{0:T(1024)(128)(4,1)S(1)} %dynamic_slice.53), kind=kOutput, calls=%fused_computation.10.clone.1 | convolution fusion | flops 5041553408 | bytes 2069508 | tf_op jit(solution)/shard_map/while/body/eval_jaxpr/dot_general | solution.py:38
  52.5 7.7 %fusion.114 = f32[100,8192]{1,0:T(8,128)S(1)} fusion(f32[100,8192]{1,0:T(8,128)S(1)} %get-tuple-element.1059, s32[]{:T(128)S(6)} %select_n.35, f32[100,4096]{1,0:T(8,128)} %get-tuple-element.1071, s32[1024]{0:T(1024)S(1)} %dynamic_slice.52, pred[1024]{0:T(1024)(128)(4,1)S(1)} %dynamic_slice.53), kind=kOutput, calls=%fused_computation.10.clone.1 | convolution fusion | flops 5041553408 | bytes 2069508 | tf_op jit(solution)/shard_map/while/body/eval_jaxpr/dot_general | solution.py:38
  60.9 7.7 %fusion.114 = f32[100,8192]{1,0:T(8,128)S(1)} fusion(f32[100,8192]{1,0:T(8,128)S(1)} %get-tuple-element.1059, s32[]{:T(128)S(6)} %select_n.35, f32[100,4096]{1,0:T(8,128)} %get-tuple-element.1071, s32[1024]{0:T(1024)S(1)} %dynamic_slice.52, pred[1024]{0:T(1024)(128)(4,1)S(1)} %dynamic_slice.53), kind=kOutput, calls=%fused_computation.10.clone.1 | convolution fusion | flops 5041553408 | bytes 2069508 | tf_op jit(solution)/shard_map/while/body/eval_jaxpr/dot_general | solution.py:38
  68.6 3.4 copy.31
  72.0 12.3 %all-to-all-start = ((f32[100,128,64]{0,2,1:T(8,128)}), f32[100,128,64]{0,2,1:T(8,128)}, u32[]{:S(2)}, u32[]{:S(2)}) async-start(f32[100,128,64]{0,2,1:T(8,128)} %bitcast.241), calls=%async_computation | async-start | bytes 8388608 | tf_op jit(solution)/shard_map/all_to_all | solution.py:71
  99.1 26.0 %slice_reduce_fusion.2 = (f32[196608]{0:T(1024)S(1)}, f32[196608]{0:T(1024)}, f32[196608]{0:T(1024)}, f32[196608]{0:T(1024)S(1)}, f32[196608]{0:T(1024)S(1)}, /*index=5*/f32[196608]{0:T(1024)}) fusion(f32[3,196608]{1,0:T(4,128)} %param.20, f32[3,196608]{1,0:T(4,128)} %param.21), kind=kLoop, calls=%fused_computation.141 | loop fusion | bytes 9437184 | tf_op jit(solution)/shard_map/slice | solution.py:13
  126.9 2.1 mul.1695
  129.0 2.2 mul.1690
  149.5 39.1 %fusion.99 = (f32[20,1,8192]{2,1,0:T(1,128)}, f32[20,1,8192]{2,1,0:T(1,128)}, f32[20,1,8192]{2,1,0:T(1,128)}, f32[20,1,8192]{2,1,0:T(1,128)}, f32[20,1,8192]{2,1...) fusion(f32[20,24,8192]{2,1,0:T(8,128)} %fusion.97), kind=kLoop, calls=%fused_computation.249 | loop fusion | bytes 24903680 | tf_op jit(solution)/shard_map/slice | solution.py:82
  188.6 12.0 %fusion.100 = (f32[20,1,8192]{2,1,0:T(1,128)S(1)}, f32[20,1,8192]{2,1,0:T(1,128)S(1)}, f32[20,1,8192]{2,1,0:T(1,128)S(1)}, f32[20,1,8192]{2,1,0:T(1,128)S(1)}, f32[20,1,8192]{2,1,0:T(1,128)S(1)}) fusion(f32[20,24,8192]{2,1,0:T(8,128)} %fusion.97), kind=kLoop, calls=%fused_computation.250 | loop fusion | bytes 6553600 | tf_op jit(solution)/shard_map/slice | solution.py:80
  208.3 1.3 copy.183
  213.5 1.3 copy.187
  214.8 1.3 copy.188
  220.0 1.3 copy.193
  221.3 1.3 copy.194
  223.9 1.3 copy.196
  225.2 1.3 copy.197
  226.5 1.3 copy.198
  231.6 4.6 fusion.102
  236.2 8.2 %copy.32 = f32[100,128,64]{2,1,0:T(8,128)} copy(f32[100,128,64]{0,2,1:T(8,128)} %all-to-all-done) | data formatting | bytes 6553600 | tf_op jit(solution)/shard_map/all_to_all | solution.py:71
  244.4 7.3 %reshape.547 = f32[5,20,8192]{2,1,0:T(8,128)} reshape(f32[100,128,64]{2,1,0:T(8,128)} %copy.32) | data formatting | bytes 6553600 | tf_op jit(solution)/shard_map/reshape | solution.py:74
  251.7 1.5 slice.473
  253.1 11.5 %fusion.101 = (f32[5,1,8192]{2,1,0:T(1,128)S(1)}, f32[5,1,8192]{2,1,0:T(1,128)S(1)}, f32[5,1,8192]{2,1,0:T(1,128)S(1)}, f32[5,1,8192]{2,1,0:T(1,128)S(1)}, f32[5...) fusion(f32[5,20,8192]{2,1,0:T(8,128)} %reshape.547), kind=kLoop, calls=%fused_computation.251 | loop fusion | bytes 6225920 | tf_op jit(solution)/shard_map/slice | solution.py:75
  274.6 11.6 %add_multiply_fusion = f32[5,24,8192]{2,0,1:T(8,128)S(1)} fusion(f32[24,8192]{1,0:T(8,128)} %mul.1778, f32[24,8192]{1,0:T(8,128)} %get-tuple-element.702, f32[5,8192]{1,0:T(8,128)} %get-tuple-element.708, f32[24,8192]{1,0:T(8,128)} %get-tuple-element.672, f32[5,8192]{1,0:T(8,128)} %get-tuple-element.709, f32[24,8192]{1,0:T(8,128)} %get-tuple-element.673, ...), kind=kLoop, calls=%fused_computation.83 | loop fusion | flops 38338560 | bytes 22937600 | tf_op jit(solution)/shard_map/mul | solution.py:78
  286.4 1.5 slice_bitcast_fusion.7
  291.5 5.6 add_add_fusion
  297.1 2.9 reshape.560
  300.0 3.5 broadcast_multiply_fusion.6
  303.5 4.3 mul.1882
  307.8 3.5 broadcast_multiply_fusion.5
  311.3 4.3 mul.1888
  315.7 3.5 broadcast_multiply_fusion.4
  319.2 4.3 mul.1894
  323.5 3.5 broadcast_multiply_fusion.3
  327.1 4.4 mul.1900
  331.4 3.6 broadcast_multiply_fusion.2
  335.0 4.3 mul.1906
  339.3 3.6 broadcast_multiply_fusion.1
  342.9 4.4 mul.1912
  347.4 3.6 broadcast_multiply_fusion
  351.0 4.3 mul.1918
  355.3 3.5 broadcast_multiply_fusion.7
  358.8 4.5 mul.1876
  363.3 12.0 %add_add_fusion.1 = f32[100,8192]{1,0:T(8,128)} fusion(f32[100,8192]{1,0:T(8,128)} %mul.1918, f32[100,8192]{1,0:T(8,128)} %mul.1912, f32[100,8192]{1,0:T(8,128)} %mul.1906, f32[100,8192]{1,0:T(8,128)} %mul.1900, f32[100,8192]{1,0:T(8,128)} %mul.1894, f32[100,8192]{1,0:T(8,128)} %mul.1888, f32[100,8192]{1,0:T(8,128)} %mul.1882, f32[100,8192]{1,0:T(8,128)S(1)} %reshape.560, ...), kind=kLoop, calls=%fused_computation.85 | loop fusion | flops 6553600 | bytes 32768000 | tf_op jit(solution)/shard_map/add | solution.py:82
  375.3 47.0 %while.44 = (s32[]{:T(128)}, f32[100,2048]{1,0:T(8,128)}, f32[100,8192]{1,0:T(8,128)}, s32[8192]{0:T(1024)}, s32[]{:T(128)}, /*index=5*/s32[]{:T(128)}, s32[]{:T(128)}, s32[]{:T(128)}) while((s32[]{:T(128)}, f32[100,2048]{1,0:T(8,128)}, f32[100,8192]{1,0:T(8,128)}, s32[8192]{0:T(1024)}, s32[]{:T(128)}, /*index=5*/s32[]{:T(128)}, ...), condition=%wide.region_3.0_spmd.clone, body=%wide.region_2.0_spmd.clone.sunk | while | flops 2519089152 | bytes 2109597 | solution.py:98
  376.0 4.9 fusion.118
  381.6 5.2 fusion.118
  387.6 5.2 fusion.118
  393.5 5.2 fusion.118
  399.4 5.2 fusion.118
  405.3 5.2 fusion.118
  411.2 5.2 fusion.118
  417.1 5.2 fusion.118
  437.9 94.3 %while.43 = (s32[]{:T(128)}, f32[100,2048]{1,0:T(8,128)}, s32[2048]{0:T(1024)}, f32[5,2048]{1,0:T(8,128)}, f32[100]{0:T(128)}, /*index=5*/f32[5,2048]{1,0:T(8,12...) while((s32[]{:T(128)}, f32[100,2048]{1,0:T(8,128)}, ...), condition=%wide.region_5.0_spmd.clone, body=%wide.region_4.0_spmd.clone.sunk | while | flops 2526871552 | bytes 67369304 | solution.py:44
  474.6 10.4 %fusion.116 = f32[100,2048]{1,0:T(8,128)} fusion(f32[100,2048]{1,0:T(8,128)} %get-tuple-element.1149, s32[]{:T(128)S(6)} %select_n.36, s32[1024]{0:T(1024)S(1)} %dynamic_slice.54, f32[100,2048]{1,0:T(8,128)S(1)} %mul.2903, f32[100,2048]{1,0:T(8,128)S(1)} %mul.2905, f32[100,2048]{1,0:T(8,128)S(1)} %mul.2907, f32[100,2048]{1,0:T(8,128)} %mul.2909, ...), kind=kOutput, calls=%fused_computation.15.clone.1 | convolution fusion | flops 2526871552 | bytes 17389460 | tf_op jit(solution)/shard_map/while/body/eval_jaxpr/dot_general | solution.py:38
  521.8 10.4 %fusion.116 = f32[100,2048]{1,0:T(8,128)} fusion(f32[100,2048]{1,0:T(8,128)} %get-tuple-element.1149, s32[]{:T(128)S(6)} %select_n.36, s32[1024]{0:T(1024)S(1)} %dynamic_slice.54, f32[100,2048]{1,0:T(8,128)S(1)} %mul.2903, f32[100,2048]{1,0:T(8,128)S(1)} %mul.2905, f32[100,2048]{1,0:T(8,128)S(1)} %mul.2907, f32[100,2048]{1,0:T(8,128)} %mul.2909, ...), kind=kOutput, calls=%fused_computation.15.clone.1 | convolution fusion | flops 2526871552 | bytes 17389460 | tf_op jit(solution)/shard_map/while/body/eval_jaxpr/dot_general | solution.py:38
  532.2 1.5 copy.53
  533.8 28.7 %all_to_all.21 = f32[100,128,16]{0,2,1:T(8,128)S(1)} all-to-all(f32[100,128,16]{0,2,1:T(8,128)S(1)} %bitcast.242), channel_id=1, replica_groups=mesh['dom'=16,'sub'=8] {'dom','sub'}, dimensions={1} | all-to-all | bytes 1638400 | tf_op jit(solution)/shard_map/all_to_all | solution.py:108
  (309 shorter events, 171.4 us)
Async XLA Ops:
  0.0 0.8 copy-start
  72.0 12.3 %copy-start.4 = (f32[20,20]{1,0:T(8,128)S(1)}, f32[20,20]{1,0:T(8,128)}, u32[]{:S(2)}) copy-start(f32[20,20]{1,0:T(8,128)} %param.24) | copy-start | bytes 4804
  72.0 26.0 %copy-start.37 = (f32[196608]{0:T(1024)S(1)}, f32[196608]{0:T(1024)}, u32[]{:S(2)}) copy-start(f32[196608]{0:T(1024)} %param.22) | copy-start | bytes 2359300
  72.0 164.2 %all-to-all-start = ((f32[100,128,64]{0,2,1:T(8,128)}), f32[100,128,64]{0,2,1:T(8,128)}, u32[]{:S(2)}, u32[]{:S(2)}) async-start(f32[100,128,64]{0,2,1:T(8,128)} %bitcast.241), calls=%async_computation | async-start | bytes 8388608 | tf_op jit(solution)/shard_map/all_to_all | solution.py:71
  188.6 13.3 %copy-start.36 = (f32[20,1,8192]{2,1,0:T(1,128)S(1)}, f32[20,1,8192]{2,1,0:T(1,128)}, u32[]{:S(2)}) copy-start(f32[20,1,8192]{2,1,0:T(1,128)} %get-tuple-element.599) | copy-start | bytes 1966084
  200.6 7.8 %copy-start.35 = (f32[20,1,8192]{2,1,0:T(1,128)S(1)}, f32[20,1,8192]{2,1,0:T(1,128)}, u32[]{:S(2)}) copy-start(f32[20,1,8192]{2,1,0:T(1,128)} %get-tuple-element.600) | copy-start | bytes 1966084
  201.9 7.8 %copy-start.34 = (f32[20,1,8192]{2,1,0:T(1,128)S(1)}, f32[20,1,8192]{2,1,0:T(1,128)}, u32[]{:S(2)}) copy-start(f32[20,1,8192]{2,1,0:T(1,128)} %get-tuple-element.601) | copy-start | bytes 1966084
  203.2 7.8 %copy-start.33 = (f32[20,1,8192]{2,1,0:T(1,128)S(1)}, f32[20,1,8192]{2,1,0:T(1,128)}, u32[]{:S(2)}) copy-start(f32[20,1,8192]{2,1,0:T(1,128)} %get-tuple-element.602) | copy-start | bytes 1966084
  204.5 7.7 %copy-start.32 = (f32[20,1,8192]{2,1,0:T(1,128)S(1)}, f32[20,1,8192]{2,1,0:T(1,128)}, u32[]{:S(2)}) copy-start(f32[20,1,8192]{2,1,0:T(1,128)} %get-tuple-element.603) | copy-start | bytes 1966084
  205.7 7.8 %copy-start.31 = (f32[20,1,8192]{2,1,0:T(1,128)S(1)}, f32[20,1,8192]{2,1,0:T(1,128)}, u32[]{:S(2)}) copy-start(f32[20,1,8192]{2,1,0:T(1,128)} %get-tuple-element.604) | copy-start | bytes 1966084
  207.0 7.8 %copy-start.30 = (f32[20,1,8192]{2,1,0:T(1,128)S(1)}, f32[20,1,8192]{2,1,0:T(1,128)}, u32[]{:S(2)}) copy-start(f32[20,1,8192]{2,1,0:T(1,128)} %get-tuple-element.605) | copy-start | bytes 1966084
  208.3 7.8 %copy-start.29 = (f32[20,1,8192]{2,1,0:T(1,128)S(1)}, f32[20,1,8192]{2,1,0:T(1,128)}, u32[]{:S(2)}) copy-start(f32[20,1,8192]{2,1,0:T(1,128)} %get-tuple-element.606) | copy-start | bytes 1966084
  209.7 7.7 %copy-start.28 = (f32[20,1,8192]{2,1,0:T(1,128)S(1)}, f32[20,1,8192]{2,1,0:T(1,128)}, u32[]{:S(2)}) copy-start(f32[20,1,8192]{2,1,0:T(1,128)} %get-tuple-element.607) | copy-start | bytes 1966084
  210.9 7.7 %copy-start.27 = (f32[20,1,8192]{2,1,0:T(1,128)S(1)}, f32[20,1,8192]{2,1,0:T(1,128)}, u32[]{:S(2)}) copy-start(f32[20,1,8192]{2,1,0:T(1,128)} %get-tuple-element.608) | copy-start | bytes 1966084
  212.2 7.7 %copy-start.26 = (f32[20,1,8192]{2,1,0:T(1,128)S(1)}, f32[20,1,8192]{2,1,0:T(1,128)}, u32[]{:S(2)}) copy-start(f32[20,1,8192]{2,1,0:T(1,128)} %get-tuple-element.609) | copy-start | bytes 1966084
  213.5 7.8 %copy-start.25 = (f32[20,1,8192]{2,1,0:T(1,128)S(1)}, f32[20,1,8192]{2,1,0:T(1,128)}, u32[]{:S(2)}) copy-start(f32[20,1,8192]{2,1,0:T(1,128)} %get-tuple-element.610) | copy-start | bytes 1966084
  216.1 7.7 %copy-start.24 = (f32[20,1,8192]{2,1,0:T(1,128)S(1)}, f32[20,1,8192]{2,1,0:T(1,128)}, u32[]{:S(2)}) copy-start(f32[20,1,8192]{2,1,0:T(1,128)} %get-tuple-element.612) | copy-start | bytes 1966084
  217.4 7.8 %copy-start.23 = (f32[20,1,8192]{2,1,0:T(1,128)S(1)}, f32[20,1,8192]{2,1,0:T(1,128)}, u32[]{:S(2)}) copy-start(f32[20,1,8192]{2,1,0:T(1,128)} %get-tuple-element.613) | copy-start | bytes 1966084
  218.7 7.8 %copy-start.22 = (f32[20,1,8192]{2,1,0:T(1,128)S(1)}, f32[20,1,8192]{2,1,0:T(1,128)}, u32[]{:S(2)}) copy-start(f32[20,1,8192]{2,1,0:T(1,128)} %get-tuple-element.614) | copy-start | bytes 1966084
  220.0 7.8 %copy-start.21 = (f32[20,1,8192]{2,1,0:T(1,128)S(1)}, f32[20,1,8192]{2,1,0:T(1,128)}, u32[]{:S(2)}) copy-start(f32[20,1,8192]{2,1,0:T(1,128)} %get-tuple-element.615) | copy-start | bytes 1966084
  223.8 7.8 %copy-start.2 = (f32[24,8192]{1,0:T(8,128)S(1)}, f32[24,8192]{1,0:T(8,128)}, u32[]{:S(2)}) copy-start(f32[24,8192]{1,0:T(8,128)} %mul.1695) | copy-start | bytes 2359300
  223.9 7.8 %copy-start.3 = (f32[24,8192]{1,0:T(8,128)S(1)}, f32[24,8192]{1,0:T(8,128)}, u32[]{:S(2)}) copy-start(f32[24,8192]{1,0:T(8,128)} %mul.1690) | copy-start | bytes 2359300
  286.1 1.7 copy-start.17
  286.2 1.8 copy-start.18
  286.2 2.3 copy-start.19
  286.2 2.6 copy-start.20
  286.3 2.7 copy-start.5
  286.3 3.0 copy-start.6
  286.3 3.2 copy-start.7
  286.3 3.4 copy-start.8
  286.3 3.6 copy-start.9
  286.3 3.9 copy-start.10
  286.3 4.1 copy-start.11
  286.4 4.3 copy-start.12
  286.4 4.5 copy-start.13
  286.4 4.7 copy-start.14
  286.4 4.9 copy-start.15
  286.4 5.1 copy-start.16
  422.3 15.5 %copy-start.38 = (f32[2048]{0:T(1024)S(1)}, f32[2048]{0:T(1024)}, u32[]{:S(2)}) copy-start(f32[2048]{0:T(1024)} %param.23) | copy-start | bytes 24580
  532.2 31.5 %copy-start.1 = (s32[128,128]{1,0:T(8,128)S(1)}, s32[128,128]{1,0:T(8,128)}, u32[]{:S(2)}) copy-start(s32[128,128]{1,0:T(8,128)} %param.18) | copy-start | bytes 196612
where the time goes:
time: 574 us; the launch traced here: 564 us
  local copies, waits for them, and re-layouts  320 us (56%)
  matrix products  124 us (22%)
  other arithmetic  77.6 us (14%)
  blocking collectives  28.7 us (5%)
  starting transfers between devices  12.3 us (2%)
    dot_general x10, matrix products, step(): jnp.dot(source, onehot, precision=lax.Precision.HIGHEST, preferred_elemen...  82.2 us
    mul x114, local copies, waits for them, and re-layouts, local(): minv_ref[None, :, mode, None] * rhs_modes[:, mode, None, :]  79.2 us
    unnamed x136, local copies, waits for them, and re-layouts  62 us
    dot_general x8, matrix products, deposit(): jnp.dot(part_moments, onehot, precision=lax.Precision.HIGHEST, preferred_...  41.5 us
    slice x1, local copies, waits for them, and re-layouts, local(): basis_new[None, :, point, :] * weighted[:, None, point, :]  39.1 us
    mul x9, local copies, waits for them, and re-layouts, local(): basis_new[None, :, point, :] * weighted[:, None, point, :]  36.5 us
    all_to_all x1, blocking collectives, local(): lax.all_to_all(leaving, ('dom', 'sub'), split_axis=1, concat_axis=1, tile...  28.7 us
    mul x8, other arithmetic, local(): basis_new[None, :, point, :] * weighted[:, None, point, :]  28.3 us
  transfers between devices with their start and end apart: 1, of which 0 were waited for; matrix products, arithmetic and copies ran while one was open for 27% of the time, Pallas kernels for 0%

commit v1 on v0

v1 whole, which is shorter than its diff:
```python
import functools
import jax
import jax.numpy as jnp
from jax import lax
from jax.experimental import pallas as pl
from jax.experimental.pallas import tpu as pltpu
from jax.sharding import PartitionSpec as P

VARS = 5
MODES = 20
ROWS = 100
HALF = 50
QUAD = 24
CAP = 64
LANES = 128


def gather_kernel(idx_ref, cnt_ref, coef_ref, out_ref, tab_ref, buf0, buf1):
    width = coef_ref.shape[1]
    pad = jnp.zeros((64 - HALF, LANES), jnp.float32)

    def build(j, carry):
        start = pl.multiple_of(j * LANES, LANES)
        block = coef_ref[:, pl.ds(start, LANES)]
        wide = jnp.concatenate([block[:HALF], pad, block[HALF:], pad], axis=0)
        tab_ref[pl.ds(start, LANES), :] = wide.T
        return carry

    lax.fori_loop(0, width // LANES, build, 0, unroll=2)
    lane = lax.broadcasted_iota(jnp.int32, (1, LANES), 1)
    low = lane < 64

    def fetch(pair, buf):
        for j in range(LANES):
            buf[pl.ds(j, 1), :] = tab_ref[pl.ds(idx_ref[pair * LANES + j], 1), :]

    def emit(pair, buf, base, shift):
        limit = jnp.where(low, cnt_ref[2 * pair], cnt_ref[2 * pair + 1] + 64)
        turned = buf[...].T
        live = lane < limit
        first = jnp.where(live, turned[:HALF], 0.0)
        second = jnp.where(live, turned[64 : 64 + HALF], 0.0)
        first_r = pltpu.roll(first, 64, 1)
        second_r = pltpu.roll(second, 64, 1)
        out_ref[pl.ds(base + shift, HALF), :] = jnp.where(low, first, second_r)
        out_ref[pl.ds(base + shift + HALF, HALF), :] = jnp.where(low, first_r, second)

    pairs = idx_ref.shape[0] // LANES
    fetch(0, buf0)

    def step(turn, carry):
        base = pl.multiple_of(turn * 200, 8)
        fetch(2 * turn + 1, buf1)
        emit(2 * turn, buf0, base, 0)
        fetch(jnp.minimum(2 * turn + 2, pairs - 1), buf0)
        emit(2 * turn + 1, buf1, base, 100)
        return carry

    lax.fori_loop(0, pairs // 2, step, 0)


def gather(old_coef, old_index, counts):
    slots = old_index.shape[0]
    width = old_coef.shape[1]
    return pl.pallas_call(
        gather_kernel,
        out_shape=jax.ShapeDtypeStruct((slots // CAP * HALF, LANES), jnp.float32),
        in_specs=[
            pl.BlockSpec(memory_space=pltpu.SMEM),
            pl.BlockSpec(memory_space=pltpu.SMEM),
            pl.BlockSpec(memory_space=pltpu.VMEM),
        ],
        out_specs=pl.BlockSpec(memory_space=pltpu.VMEM),
        scratch_shapes=[
            pltpu.VMEM((width, LANES), jnp.float32),
            pltpu.VMEM((LANES, LANES), jnp.float32),
            pltpu.VMEM((LANES, LANES), jnp.float32),
        ],
        name="gather",
    )(old_index, counts, old_coef)


def monomials(first, second, third):
    unit = None
    fp = [unit, first, first * first]
    fp.append(fp[2] * first)
    sp = [unit, second, second * second]
    sp.append(sp[2] * second)
    tp = [unit, third, third * third]
    tp.append(tp[2] * third)
    rows = []
    for degree in range(4):
        for a in range(degree, -1, -1):
            for b in range(degree - a, -1, -1):
                out = None
                for term in (fp[a], sp[b], tp[degree - a - b]):
                    if term is not None:
                        out = term if out is None else out * term
                rows.append(out)
    return rows


def moment_kernel(old_ref, new_ref, w_ref, out_ref, po_ref, pn_ref):
    def basis(q, carry):
        weight = w_ref[q]
        old = monomials(old_ref[0, q], old_ref[1, q], old_ref[2, q])
        new = monomials(new_ref[0, q], new_ref[1, q], new_ref[2, q])
        for k in range(MODES):
            po_ref[q, k] = weight if k == 0 else old[k] * weight
            if k > 0:
                pn_ref[q, k] = new[k]
        return carry

    lax.fori_loop(0, QUAD, basis, 0)
    tile = 5
    zero = jnp.zeros((8, LANES), jnp.float32)
    for m0 in range(0, MODES, tile):
        for k0 in range(0, MODES, tile):

            def add(q, accs):
                left = [None if m0 + i == 0 else pn_ref[q, m0 + i] for i in range(tile)]
                right = [po_ref[q, k0 + j] for j in range(tile)]
                return tuple(
                    accs[i * tile + j] + (right[j] if left[i] is None else left[i] * right[j])
                    for i in range(tile)
                    for j in range(tile)
                )

            accs = lax.fori_loop(0, QUAD, add, (zero,) * (tile * tile), unroll=4)
            for i in range(tile):
                for j in range(tile):
                    out_ref[0, (m0 + i) * MODES + k0 + j] = accs[i * tile + j]


def moment_matrix(old_points, new_points, weights):
    groups = weights.shape[0] // QUAD // LANES
    blocks = groups // 8
    shape = (3, QUAD, groups, LANES)
    return pl.pallas_call(
        moment_kernel,
        grid=(blocks,),
        out_shape=jax.ShapeDtypeStruct((blocks, MODES * MODES, 8, LANES), jnp.float32),
        in_specs=[
            pl.BlockSpec((3, QUAD, 8, LANES), lambda i: (0, 0, i, 0)),
            pl.BlockSpec((3, QUAD, 8, LANES), lambda i: (0, 0, i, 0)),
            pl.BlockSpec((QUAD, 8, LANES), lambda i: (0, i, 0)),
        ],
        out_specs=pl.BlockSpec((1, MODES * MODES, 8, LANES), lambda i: (i, 0, 0, 0)),
        scratch_shapes=[
            pltpu.VMEM((QUAD, MODES, 8, LANES), jnp.float32),
            pltpu.VMEM((QUAD, MODES, 8, LANES), jnp.float32),
        ],
        cost_estimate=pl.CostEstimate(
            flops=int(20e-6 * 1.1e15), bytes_accessed=40 * 2**20, transcendentals=0
        ),
        name="moment_matrix",
    )(old_points.reshape(shape), new_points.reshape(shape), weights.reshape(shape[1:]))


def index_kernel(order_s, index_ref, jac_ref, target_ref, jacp_ref, order_ref):
    rows = jac_ref.shape[0]
    place = lax.broadcasted_iota(jnp.int32, (rows, LANES), 0) * LANES + lax.broadcasted_iota(
        jnp.int32, (rows, LANES), 1
    )

    def invert(p, inverse):
        return jnp.where(place == order_s[p], p, inverse)

    inverse = lax.fori_loop(
        0, rows * LANES, invert, jnp.zeros((rows, LANES), jnp.int32), unroll=8
    )

    def look(table, index):
        low = index & (LANES - 1)
        high = index >> 7
        found = jnp.zeros(index.shape, table.dtype)
        for r in range(rows):
            row = jnp.broadcast_to(table[r : r + 1], index.shape)
            found = jnp.where(high == r, jnp.take_along_axis(row, low, axis=1), found)
        return found

    for g in range(index_ref.shape[0] // 8):
        target_ref[8 * g : 8 * g + 8, :] = look(inverse, index_ref[8 * g : 8 * g + 8, :])
    jac = jac_ref[...]
    for g in range(rows // 8):
        jacp_ref[8 * g : 8 * g + 8, :] = look(jac, order_ref[8 * g : 8 * g + 8, :])


def index_tables(order, new_index, jacobian):
    slots = new_index.shape[0]
    count = order.shape[0]
    vm = pl.BlockSpec(memory_space=pltpu.VMEM)
    return pl.pallas_call(
        lambda s, i, j, o, t, jp: index_kernel(s, i, j, t, jp, o),
        out_shape=(
            jax.ShapeDtypeStruct((slots // LANES, LANES), jnp.int32),
            jax.ShapeDtypeStruct((count // LANES, LANES), jnp.float32),
        ),
        in_specs=[pl.BlockSpec(memory_space=pltpu.SMEM), vm, vm, vm],
        out_specs=(vm, vm),
        cost_estimate=pl.CostEstimate(
            flops=int(4e-6 * 1.1e15), bytes_accessed=8 * 2**20, transcendentals=0
        ),
        name="index_tables",
    )(
        order,
        new_index.reshape(-1, LANES),
        jacobian.reshape(-1, LANES),
        order.reshape(-1, LANES),
    )


PADF = 104
BINS = 512


def project_kernel(
    recv_ref, m_ref, target_ref, minv_ref, jac_ref, out_ref, coef_ref, y_ref, lhs_ref, acc_ref
):
    turn = pl.program_id(0)
    folds = acc_ref.shape[0] // (2 * PADF)

    @pl.when(turn == 0)
    def _():
        acc_ref[...] = jnp.zeros_like(acc_ref)
        y_ref[...] = jnp.zeros_like(y_ref)

    lane = lax.broadcasted_iota(jnp.int32, (8, LANES), 1)
    low = lane < 64
    for r in range(HALF):
        even = recv_ref[pl.ds(r, 8, stride=2 * HALF), :]
        odd = recv_ref[pl.ds(HALF + r, 8, stride=2 * HALF), :]
        coef_ref[r] = jnp.where(low, even, pltpu.roll(odd, 64, 1))
        coef_ref[r + HALF] = jnp.where(low, pltpu.roll(even, 64, 1), odd)
    tile = 4
    for m0 in range(0, MODES, tile):
        accs = [None] * (tile * VARS)
        for k in range(MODES):
            coefs = [coef_ref[v * MODES + k] for v in range(VARS)]
            for i in range(tile):
                entry = m_ref[0, (m0 + i) * MODES + k]
                for v in range(VARS):
                    term = entry * coefs[v]
                    old = accs[i * VARS + v]
                    accs[i * VARS + v] = term if old is None else old + term
        for i in range(tile):
            for v in range(VARS):
                f = v * MODES + m0 + i
                y_ref[pl.ds((f // 8) * 64 + f % 8, 8, stride=8), :] = accs[i * VARS + v]
    slots = 8 * LANES
    rows = []
    for fb in range(PADF // 8):
        rows.append(
            jnp.concatenate(
                [y_ref[(fb * 8 + g) * 8 : (fb * 8 + g) * 8 + 8, :] for g in range(8)], axis=1
            )
        )
    y = jnp.concatenate(rows, axis=0)
    high = y.astype(jnp.bfloat16)
    rest = y - high.astype(jnp.float32)
    both = jnp.concatenate([high.astype(jnp.float32), rest], axis=0).astype(jnp.bfloat16)
    target = jnp.concatenate([target_ref[g : g + 1, :] for g in range(8)], axis=1)
    fold = target // BINS
    for a in range(folds):
        keep = jnp.where(fold == a, 1.0, 0.0).astype(jnp.bfloat16)
        lhs_ref[a * 2 * PADF : (a + 1) * 2 * PADF, :] = both * keep
    bins = lax.broadcasted_iota(jnp.int32, (BINS, slots), 0)
    onehot = jnp.where(bins == (target & (BINS - 1)), 1.0, 0.0).astype(jnp.bfloat16)
    acc_ref[...] += lax.dot_general(
        lhs_ref[...], onehot, (((1,), (1,)), ((), ())), preferred_element_type=jnp.float32
    )

    @pl.when(turn == pl.num_programs(0) - 1)
    def _():
        for a in range(folds):
            base = a * 2 * PADF
            rhs = acc_ref[base : base + PADF, :] + acc_ref[base + PADF : base + 2 * PADF, :]
            done = jnp.dot(
                minv_ref[...],
                rhs,
                precision=lax.Precision.HIGHEST,
                preferred_element_type=jnp.float32,
            )
            done = done / jac_ref[:, a * BINS : (a + 1) * BINS]
            for j in range(BINS // LANES):
                out_ref[a * BINS + j * LANES : a * BINS + (j + 1) * LANES, :] = done[
                    :, j * LANES : (j + 1) * LANES
                ].T


def project(received, matrix, target, minv, jac):
    blocks = matrix.shape[0]
    count = jac.shape[1]
    rows = received.shape[0] // blocks
    folds = count // BINS
    return pl.pallas_call(
        project_kernel,
        grid=(blocks,),
        out_shape=jax.ShapeDtypeStruct((count, LANES), jnp.float32),
        in_specs=[
            pl.BlockSpec((rows, LANES), lambda i: (i, 0)),
            pl.BlockSpec((1, MODES * MODES, 8, LANES), lambda i: (i, 0, 0, 0)),
            pl.BlockSpec((8, LANES), lambda i: (i, 0)),
            pl.BlockSpec((LANES, PADF), lambda i: (0, 0)),
            pl.BlockSpec((1, count), lambda i: (0, 0)),
        ],
        out_specs=pl.BlockSpec((count, LANES), lambda i: (0, 0)),
        scratch_shapes=[
            pltpu.VMEM((ROWS, 8, LANES), jnp.float32),
            pltpu.VMEM((PADF * 8, LANES), jnp.float32),
            pltpu.VMEM((folds * 2 * PADF, 8 * LANES), jnp.bfloat16),
            pltpu.VMEM((folds * 2 * PADF, BINS), jnp.float32),
        ],
        name="project",
    )(received, matrix, target, minv, jac)


def local(old_coef, old_index, pair_count, new_index, old_points, new_points, weights, jacobian,
          minv_ref, send_order):
    axes = ("dom", "sub")
    devices = lax.axis_size(axes)
    myself = lax.axis_index(axes)
    counts = lax.dynamic_slice_in_dim(pair_count, myself, 1, 0)[0]
    outgoing = gather(old_coef, old_index, counts)
    outgoing = outgoing.reshape(devices, HALF // 2, 2, LANES)
    received = lax.all_to_all(outgoing, axes, split_axis=0, concat_axis=0, tiled=True)
    received = received.reshape(devices * HALF, LANES)
    matrix = moment_matrix(old_points, new_points, weights)
    target, jac = index_tables(send_order[0], new_index, jacobian)
    minv = jnp.pad(jnp.kron(jnp.eye(VARS, dtype=jnp.float32), minv_ref), ((0, 28), (0, 4)))
    leaving = project(received, matrix, target, minv, jac.reshape(1, -1))
    leaving = leaving.reshape(devices, -1, LANES)
    arrived = lax.all_to_all(leaving, axes, split_axis=0, concat_axis=0, tiled=True)
    return arrived.reshape(-1, LANES)[:, :ROWS].T


def solution(mesh):
    placed = (
        P(None, ("dom", "sub")),
        P(("dom", "sub")),
        P(),
        P(("dom", "sub")),
        P(None, ("dom", "sub")),
        P(None, ("dom", "sub")),
        P(("dom", "sub")),
        P(("dom", "sub")),
        P(),
        P(("dom", "sub"), None),
    )
    return jax.shard_map(
        local, mesh=mesh, in_specs=placed, out_specs=P(None, ("dom", "sub")), check_vma=False
    )
```

time: 574 us -> 123 us (0.21); the launches traced: 564 us -> 123 us
  local copies, waits for them, and re-layouts: 320 us -> 11.3 us
  matrix products: 124 us -> 0 us
  other arithmetic: 77.6 us -> 0.85 us
  Pallas kernels: 0 us -> 70 us
    mul x134 -> x1, local copies, waits for them, and re-layouts: 126 us -> 1.12 us  [local(): jnp.kron(jnp.eye(VARS, dtype=jnp.float32), minv_ref)]
    dot_general x18 -> x0, matrix products: 124 us -> none  [the longest x10 82.2 us: step(): jnp.dot(source, onehot, precision=lax.Precision.HIGHEST, preferred_elemen...]
    slice x12 -> x0, local copies, waits for them, and re-layouts: 92.9 us -> none  [the longest x1 39.1 us: local(): basis_new[None, :, point, :] * weighted[:, None, point, :]]
    pallas_call x0 -> x4, Pallas kernels: none -> 70 us  [the longest x1 30.8 us: moment_matrix(): pl.pallas_call(moment_kernel, grid=(blocks,), out_shape=jax.ShapeDtypeStr...]
    unnamed x136 -> x10, local copies, waits for them, and re-layouts: 62 us -> 7.7 us
    mul x10 -> x1, other arithmetic: 44.5 us -> 0.85 us  [local(): jnp.kron(jnp.eye(VARS, dtype=jnp.float32), minv_ref)]
    add x2 -> x0, other arithmetic: 17.6 us -> none  [local(): moments + basis_new[None, :, point, :] * weighted[:, None, point, :]]
    unnamed x16 -> x0, other arithmetic: 14.5 us -> none
  transfers between devices with their start and end apart: 1 -> 1, of which waited for: 0 -> 0; matrix products, arithmetic and copies ran while one was open for 27% -> 6% of each run, Pallas kernels for 0% -> 29%
where the time goes in v1:
time: 123 us
  Pallas kernels  70 us (57%)
  blocking collectives  28.9 us (23%)
  starting transfers between devices  11.5 us (9%)
  local copies, waits for them, and re-layouts  11.3 us (9%)
    pallas_call x1, Pallas kernels, moment_matrix(): pl.pallas_call(moment_kernel, grid=(blocks,), out_shape=jax.ShapeDtypeStr...  30.8 us
    all_to_all x1, blocking collectives, local(): lax.all_to_all(leaving, axes, split_axis=0, concat_axis=0, tiled=True)  28.9 us
    pallas_call x1, Pallas kernels, project(): pl.pallas_call(project_kernel, grid=(blocks,), out_shape=jax.ShapeDtypeSt...  18 us
    pallas_call x1, Pallas kernels, gather(): pl.pallas_call(gather_kernel, out_shape=jax.ShapeDtypeStruct((slots // CA...  16.7 us
    all_to_all x1, starting transfers between devices, local(): lax.all_to_all(outgoing, axes, split_axis=0, concat_axis=0, tiled=True)  11.5 us
    unnamed x10, local copies, waits for them, and re-layouts  7.7 us
    pallas_call x1, Pallas kernels, index_tables(): pl.pallas_call(lambda s, i, j, o, t, jp: index_kernel(s, i, j, t, jp, o),...  4.48 us
  transfers between devices with their start and end apart: 1, of which 0 were waited for; matrix products, arithmetic and copies ran while one was open for 6% of the time, Pallas kernels for 29%

profile of v1, /device:TPU:1, one launch (start us, length us, event | category | flops | bytes accessed | tf_op | source)
XLA Modules:
  0.0 122.6 jit_solution(11202309478110489684)
XLA Ops:
  0.0 0.0 copy-start
  0.0 0.8 copy-done
  0.8 0.5 dynamic-slice_bitcast_fusion.cnt_ref
  1.4 16.7 %gather.1 = f32[6400,128]{1,0:T(8,128)} custom-call(s32[8192]{0:T(1024)} %idx_ref.1, s32[128]{0:T(128)} %dynamic-slice_bitcast_fusion.cnt_ref, f32[100,4096]{1,0:T(8,128)} %coef_ref.1), custom_call_target="tpu_custom_call" | custom-call | tf_op jit(solution)/shard_map/gather/pallas_call | solution.py:65
  18.1 11.5 %all-to-all-start = ((f32[128,25,2,128]{3,2,1,0:T(2,128)}), f32[128,25,2,128]{3,2,1,0:T(2,128)S(1)}, u32[]{:S(2)}, u32[]{:S(2)}) async-start(f32[128,25,2,128]{3,2,1,0:T(2,128)} %bitcast.20), calls=%async_computation | async-start | bytes 6553600 | tf_op jit(solution)/shard_map/all_to_all | solution.py:326
  29.6 0.0 copy-start.2
  29.6 3.6 %copy.13 = f32[1,3,1536,128]{3,2,1,0:T(8,128)} copy(f32[1,3,1536,128]{3,1,2,0:T(4,128)} %bitcast.24) | data formatting | bytes 4718592
  33.2 0.0 copy-start.3
  33.2 0.0 copy-done.2
  33.2 1.6 %copy.14 = f32[1,3,1536,128]{3,2,1,0:T(8,128)} copy(f32[1,3,1536,128]{3,1,2,0:T(4,128)S(1)} %bitcast.25) | data formatting | bytes 4718592
  34.8 0.0 copy-done.3
  34.8 0.8 broadcast_multiply_fusion
  35.6 1.1 mul.31
  36.8 0.6 pad.4.minv_ref
  37.4 4.5 %index_tables.1 = (s32[64,128]{1,0:T(8,128)}, f32[16,128]{1,0:T(8,128)}) custom-call(s32[2048]{0:T(1024)} %bitcast.31, s32[64,128]{1,0:T(8,128)} %bitcast.30, f32[16,128]{1,0:T(8,128)} %bitcast.33, s32[16,128]{1,0:T(8,128)} %bitcast.32), custom_call_target="tpu_custom_call" | custom-call | flops 4400000000 | bytes 8388608 | tf_op jit(solution)/shard_map/index_tables/pallas_call | solution.py:193
  41.9 30.8 %moment_matrix.1.m_ref = f32[8,400,8,128]{3,2,1,0:T(8,128)} custom-call(f32[3,24,64,128]{3,2,1,0:T(8,128)} %bitcast.26, f32[3,24,64,128]{3,2,1,0:T(8,128)} %bitcast.27, f32[24,64,128]{2,1,0:T(8,128)} %bitcast.29), custom_call_target="tpu_custom_call" | custom-call | flops 22000001024 | bytes 41943040 | tf_op jit(solution)/shard_map/moment_matrix/pallas_call | solution.py:139
  72.7 0.0 all-to-all-done
  72.7 0.0 copy-start.1
  72.7 1.7 %copy-done.1 = f32[128,25,2,128]{3,2,1,0:T(2,128)} copy-done((f32[128,25,2,128]{3,2,1,0:T(2,128)}, f32[128,25,2,128]{3,2,1,0:T(2,128)S(1)}, u32[]{:S(2)}) %copy-start.1) | copy-done | bytes 3276824
  74.4 18.0 %project.1 = f32[2048,128]{1,0:T(8,128)} custom-call(f32[6400,128]{1,0:T(8,128)} %bitcast.21, f32[8,400,8,128]{3,2,1,0:T(8,128)} %moment_matrix.1.m_ref, s32[64,128]{1,0:T(8,128)} %get-tuple-element.7.target_ref, f32[128,104]{1,0:T(8,128)} %pad.4.minv_ref, f32[1,2048]{1,0:T(1,128)} %bitcast.28), custom_call_target="tpu_custom_call" | custom-call | tf_op jit(solution)/shard_map/project/pallas_call | solution.py:296
  92.4 28.9 %all_to_all.10 = f32[128,16,128]{2,1,0:T(8,128)S(1)} all-to-all(f32[128,16,128]{2,1,0:T(8,128)} %bitcast.23), channel_id=1, replica_groups=mesh['dom'=16,'sub'=8] {'dom','sub'}, dimensions={0} | all-to-all | bytes 2097152 | tf_op jit(solution)/shard_map/all_to_all | solution.py:333
  121.3 0.1 slice_bitcast_fusion
  121.4 1.3 %copy.12 = f32[100,2048]{1,0:T(8,128)} copy(f32[100,2048]{0,1:T(8,128)S(1)} %slice_bitcast_fusion) | data formatting | bytes 1638400 | tf_op jit(solution)/shard_map/transpose | solution.py:334
  (1 shorter events, 0.0 us)
Async XLA Ops:
  0.0 0.8 copy-start
  18.1 54.6 %all-to-all-start = ((f32[128,25,2,128]{3,2,1,0:T(2,128)}), f32[128,25,2,128]{3,2,1,0:T(2,128)S(1)}, u32[]{:S(2)}, u32[]{:S(2)}) async-start(f32[128,25,2,128]{3,2,1,0:T(2,128)} %bitcast.20), calls=%async_computation | async-start | bytes 6553600 | tf_op jit(solution)/shard_map/all_to_all | solution.py:326
  29.6 3.6 %copy-start.2 = (f32[3,196608]{1,0:T(4,128)S(1)}, f32[3,196608]{1,0:T(4,128)}, u32[]{:S(2)}) copy-start(f32[3,196608]{1,0:T(4,128)} %param.15) | copy-start | bytes 7077892
  33.2 1.6 %copy-start.3 = (f32[20,20]{1,0:T(8,128)S(1)}, f32[20,20]{1,0:T(8,128)}, u32[]{:S(2)}) copy-start(f32[20,20]{1,0:T(8,128)} %param.18) | copy-start | bytes 4804
  72.7 1.7 %copy-start.1 = (f32[128,25,2,128]{3,2,1,0:T(2,128)}, f32[128,25,2,128]{3,2,1,0:T(2,128)S(1)}, u32[]{:S(2)}) copy-start(f32[128,25,2,128]{3,2,1,0:T(2,128)S(1)} %all-to-all-done) | copy-start | bytes 9830404

commit v2 on v1

--- a/solution.py
+++ b/solution.py
@@ -15,66 +15,65 @@
 LANES = 128
 
 
-def gather_kernel(idx_ref, cnt_ref, coef_ref, out_ref, tab_ref, buf0, buf1):
+def gather_kernel(idx_ref, cnt_ref, coef_ref, out_ref, tab_ref, buf_ref):
+    part = pl.program_id(0)
     width = coef_ref.shape[1]
-    pad = jnp.zeros((64 - HALF, LANES), jnp.float32)
-
-    def build(j, carry):
-        start = pl.multiple_of(j * LANES, LANES)
-        block = coef_ref[:, pl.ds(start, LANES)]
-        wide = jnp.concatenate([block[:HALF], pad, block[HALF:], pad], axis=0)
-        tab_ref[pl.ds(start, LANES), :] = wide.T
-        return carry
-
-    lax.fori_loop(0, width // LANES, build, 0, unroll=2)
+    pairs = buf_ref.shape[0] // LANES
     lane = lax.broadcasted_iota(jnp.int32, (1, LANES), 1)
     low = lane < 64
 
-    def fetch(pair, buf):
+    @pl.when(part == 0)
+    def _():
+        pad = jnp.zeros((64 - HALF, LANES), jnp.float32)
+
+        def build(j, carry):
+            start = pl.multiple_of(j * LANES, LANES)
+            block = coef_ref[:, pl.ds(start, LANES)]
+            wide = jnp.concatenate([block[:HALF], pad, block[HALF:], pad], axis=0)
+            tab_ref[pl.ds(start, LANES), :] = wide.T
+            return carry
+
+        lax.fori_loop(0, width // LANES, build, 0, unroll=4)
+
+    def fetch(t, carry):
+        base = pl.multiple_of(t * LANES, LANES)
+        first = (part * pairs + t) * LANES
         for j in range(LANES):
-            buf[pl.ds(j, 1), :] = tab_ref[pl.ds(idx_ref[pair * LANES + j], 1), :]
-
-    def emit(pair, buf, base, shift):
+            buf_ref[pl.ds(base + j, 1), :] = tab_ref[pl.ds(idx_ref[first + j], 1), :]
+        return carry
+
+    lax.fori_loop(0, pairs, fetch, 0)
+
+    turned = [buf_ref[u * LANES : (u + 1) * LANES, :].T for u in range(pairs)]
+    for u in range(pairs):
+        pair = part * pairs + u
         limit = jnp.where(low, cnt_ref[2 * pair], cnt_ref[2 * pair + 1] + 64)
-        turned = buf[...].T
         live = lane < limit
-        first = jnp.where(live, turned[:HALF], 0.0)
-        second = jnp.where(live, turned[64 : 64 + HALF], 0.0)
-        first_r = pltpu.roll(first, 64, 1)
-        second_r = pltpu.roll(second, 64, 1)
-        out_ref[pl.ds(base + shift, HALF), :] = jnp.where(low, first, second_r)
-        out_ref[pl.ds(base + shift + HALF, HALF), :] = jnp.where(low, first_r, second)
-
-    pairs = idx_ref.shape[0] // LANES
-    fetch(0, buf0)
-
-    def step(turn, carry):
-        base = pl.multiple_of(turn * 200, 8)
-        fetch(2 * turn + 1, buf1)
-        emit(2 * turn, buf0, base, 0)
-        fetch(jnp.minimum(2 * turn + 2, pairs - 1), buf0)
-        emit(2 * turn + 1, buf1, base, 100)
-        return carry
-
-    lax.fori_loop(0, pairs // 2, step, 0)
-
-
-def gather(old_coef, old_index, counts):
+        first = jnp.where(live, turned[u][:HALF], 0.0)
+        second = jnp.where(live, turned[u][64 : 64 + HALF], 0.0)
+        out_ref[u * ROWS : u * ROWS + HALF, :] = jnp.where(low, first, pltpu.roll(second, 64, 1))
+        out_ref[u * ROWS + HALF : (u + 1) * ROWS, :] = jnp.where(
+            low, pltpu.roll(first, 64, 1), second
+        )
+
+
+def gather(old_coef, old_index, counts, steps=4):
     slots = old_index.shape[0]
-    width = old_coef.shape[1]
+    rows, width = old_coef.shape
+    total = slots // CAP * HALF
     return pl.pallas_call(
         gather_kernel,
-        out_shape=jax.ShapeDtypeStruct((slots // CAP * HALF, LANES), jnp.float32),
+        grid=(steps,),
+        out_shape=jax.ShapeDtypeStruct((total, LANES), jnp.float32),
         in_specs=[
             pl.BlockSpec(memory_space=pltpu.SMEM),
             pl.BlockSpec(memory_space=pltpu.SMEM),
-            pl.BlockSpec(memory_space=pltpu.VMEM),
-        ],
-        out_specs=pl.BlockSpec(memory_space=pltpu.VMEM),
+            pl.BlockSpec((rows, width), lambda i: (0, 0), pipeline_mode=pl.Buffered(1)),
+        ],
+        out_specs=pl.BlockSpec((total // steps, LANES), lambda i: (i, 0)),
         scratch_shapes=[
             pltpu.VMEM((width, LANES), jnp.float32),
-            pltpu.VMEM((LANES, LANES), jnp.float32),
-            pltpu.VMEM((LANES, LANES), jnp.float32),
+            pltpu.VMEM((slots // steps, LANES), jnp.float32),
         ],
         name="gather",
     )(old_index, counts, old_coef)
@@ -103,30 +102,39 @@
 def moment_kernel(old_ref, new_ref, w_ref, out_ref, po_ref, pn_ref):
     def basis(q, carry):
         weight = w_ref[q]
-        old = monomials(old_ref[0, q], old_ref[1, q], old_ref[2, q])
-        new = monomials(new_ref[0, q], new_ref[1, q], new_ref[2, q])
-        for k in range(MODES):
-            po_ref[q, k] = weight if k == 0 else old[k] * weight
-            if k > 0:
-                pn_ref[q, k] = new[k]
+        old = monomials(*[old_ref[a, q] for a in range(3)])
+        new = monomials(*[new_ref[a, q] for a in range(3)])
+        for k in range(1, MODES):
+            pn_ref[q, k] = new[k] * weight
+            if k > 3:
+                po_ref[q, k] = old[k]
         return carry
 
-    lax.fori_loop(0, QUAD, basis, 0)
+    lax.fori_loop(0, QUAD, basis, 0, unroll=2)
     tile = 5
     zero = jnp.zeros((8, LANES), jnp.float32)
+
+    def weighted(q, m):
+        return w_ref[q] if m == 0 else pn_ref[q, m]
+
+    def plain(q, k):
+        if k == 0:
+            return None
+        return old_ref[k - 1, q] if k < 4 else po_ref[q, k]
+
     for m0 in range(0, MODES, tile):
         for k0 in range(0, MODES, tile):
 
             def add(q, accs):
-                left = [None if m0 + i == 0 else pn_ref[q, m0 + i] for i in range(tile)]
-                right = [po_ref[q, k0 + j] for j in range(tile)]
+                left = [weighted(q, m0 + i) for i in range(tile)]
+                right = [plain(q, k0 + j) for j in range(tile)]
                 return tuple(
-                    accs[i * tile + j] + (right[j] if left[i] is None else left[i] * right[j])
+                    accs[i * tile + j] + (left[i] if right[j] is None else left[i] * right[j])
                     for i in range(tile)
                     for j in range(tile)
                 )
 
-            accs = lax.fori_loop(0, QUAD, add, (zero,) * (tile * tile), unroll=4)
+            accs = lax.fori_loop(0, QUAD, add, (zero,) * (tile * tile), unroll=12)
             for i in range(tile):
                 for j in range(tile):
                     out_ref[0, (m0 + i) * MODES + k0 + j] = accs[i * tile + j]
@@ -157,7 +165,10 @@
     )(old_points.reshape(shape), new_points.reshape(shape), weights.reshape(shape[1:]))
 
 
-def index_kernel(order_s, index_ref, jac_ref, target_ref, jacp_ref, order_ref):
+def index_kernel(order_s, index_ref, jac_ref, order_ref, minv_ref, target_ref, jacp_ref, wide_ref):
+    wide_ref[...] = jnp.zeros_like(wide_ref)
+    for v in range(VARS):
+        wide_ref[v * MODES : (v + 1) * MODES, v * MODES : (v + 1) * MODES] = minv_ref[...]
     rows = jac_ref.shape[0]
     place = lax.broadcasted_iota(jnp.int32, (rows, LANES), 0) * LANES + lax.broadcasted_iota(
         jnp.int32, (rows, LANES), 1
@@ -186,18 +197,19 @@
         jacp_ref[8 * g : 8 * g + 8, :] = look(jac, order_ref[8 * g : 8 * g + 8, :])
 
 
-def index_tables(order, new_index, jacobian):
+def index_tables(order, new_index, jacobian, minv):
     slots = new_index.shape[0]
     count = order.shape[0]
     vm = pl.BlockSpec(memory_space=pltpu.VMEM)
     return pl.pallas_call(
-        lambda s, i, j, o, t, jp: index_kernel(s, i, j, t, jp, o),
+        index_kernel,
         out_shape=(
             jax.ShapeDtypeStruct((slots // LANES, LANES), jnp.int32),
             jax.ShapeDtypeStruct((count // LANES, LANES), jnp.float32),
+            jax.ShapeDtypeStruct((LANES, PADF), jnp.float32),
         ),
-        in_specs=[pl.BlockSpec(memory_space=pltpu.SMEM), vm, vm, vm],
-        out_specs=(vm, vm),
+        in_specs=[pl.BlockSpec(memory_space=pltpu.SMEM), vm, vm, vm, vm],
+        out_specs=(vm, vm, vm),
         cost_estimate=pl.CostEstimate(
             flops=int(4e-6 * 1.1e15), bytes_accessed=8 * 2**20, transcendentals=0
         ),
@@ -207,6 +219,7 @@
         new_index.reshape(-1, LANES),
         jacobian.reshape(-1, LANES),
         order.reshape(-1, LANES),
+        minv,
     )
 
 
@@ -219,17 +232,19 @@
 ):
     turn = pl.program_id(0)
     folds = acc_ref.shape[0] // (2 * PADF)
+    half = jnp.bfloat16
+    single = jnp.float32
 
     @pl.when(turn == 0)
     def _():
         acc_ref[...] = jnp.zeros_like(acc_ref)
         y_ref[...] = jnp.zeros_like(y_ref)
 
-    lane = lax.broadcasted_iota(jnp.int32, (8, LANES), 1)
-    low = lane < 64
+    low = lax.broadcasted_iota(jnp.int32, (8, LANES), 1) < 64
+    first = pl.multiple_of(turn * (8 * ROWS), 8)
     for r in range(HALF):
-        even = recv_ref[pl.ds(r, 8, stride=2 * HALF), :]
-        odd = recv_ref[pl.ds(HALF + r, 8, stride=2 * HALF), :]
+        even = recv_ref[pl.ds(first + r, 8, stride=ROWS), :]
+        odd = recv_ref[pl.ds(first + HALF + r, 8, stride=ROWS), :]
         coef_ref[r] = jnp.where(low, even, pltpu.roll(odd, 64, 1))
         coef_ref[r + HALF] = jnp.where(low, pltpu.roll(even, 64, 1), odd)
     tile = 4
@@ -256,32 +271,39 @@
             )
         )
     y = jnp.concatenate(rows, axis=0)
-    high = y.astype(jnp.bfloat16)
-    rest = y - high.astype(jnp.float32)
-    both = jnp.concatenate([high.astype(jnp.float32), rest], axis=0).astype(jnp.bfloat16)
+    high = y.astype(half).astype(single)
+    both = jnp.concatenate([high, y - high], axis=0).astype(half)
     target = jnp.concatenate([target_ref[g : g + 1, :] for g in range(8)], axis=1)
     fold = target // BINS
     for a in range(folds):
-        keep = jnp.where(fold == a, 1.0, 0.0).astype(jnp.bfloat16)
+        keep = jnp.where(fold == a, 1.0, 0.0).astype(half)
         lhs_ref[a * 2 * PADF : (a + 1) * 2 * PADF, :] = both * keep
-    bins = lax.broadcasted_iota(jnp.int32, (BINS, slots), 0)
-    onehot = jnp.where(bins == (target & (BINS - 1)), 1.0, 0.0).astype(jnp.bfloat16)
+    bins = lax.broadcasted_iota(jnp.int32, (256, slots), 0).astype(single).astype(half)
+    within = target & (BINS - 1)
+    parts = []
+    for h in range(BINS // 256):
+        wanted = (within - 256 * h).astype(single).astype(half)
+        parts.append(jnp.where(bins == wanted, jnp.array(1, half), jnp.array(0, half)))
     acc_ref[...] += lax.dot_general(
-        lhs_ref[...], onehot, (((1,), (1,)), ((), ())), preferred_element_type=jnp.float32
+        lhs_ref[...],
+        jnp.concatenate(parts, axis=0),
+        (((1,), (1,)), ((), ())),
+        preferred_element_type=single,
     )
 
     @pl.when(turn == pl.num_programs(0) - 1)
     def _():
+        minv = minv_ref[...]
+        minv_h = minv.astype(half).astype(single)
+        left = jnp.concatenate([minv_h, minv_h, minv - minv_h], axis=1).astype(half)
+        scale = 1.0 / jac_ref[...]
         for a in range(folds):
             base = a * 2 * PADF
             rhs = acc_ref[base : base + PADF, :] + acc_ref[base + PADF : base + 2 * PADF, :]
-            done = jnp.dot(
-                minv_ref[...],
-                rhs,
-                precision=lax.Precision.HIGHEST,
-                preferred_element_type=jnp.float32,
-            )
-            done = done / jac_ref[:, a * BINS : (a + 1) * BINS]
+            rhs_h = rhs.astype(half).astype(single)
+            right = jnp.concatenate([rhs_h, rhs - rhs_h, rhs_h], axis=0).astype(half)
+            done = jnp.dot(left, right, preferred_element_type=single)
+            done = done * scale[:, a * BINS : (a + 1) * BINS]
             for j in range(BINS // LANES):
                 out_ref[a * BINS + j * LANES : a * BINS + (j + 1) * LANES, :] = done[
                     :, j * LANES : (j + 1) * LANES
@@ -291,14 +313,13 @@
 def project(received, matrix, target, minv, jac):
     blocks = matrix.shape[0]
     count = jac.shape[1]
-    rows = received.shape[0] // blocks
     folds = count // BINS
     return pl.pallas_call(
         project_kernel,
         grid=(blocks,),
         out_shape=jax.ShapeDtypeStruct((count, LANES), jnp.float32),
         in_specs=[
-            pl.BlockSpec((rows, LANES), lambda i: (i, 0)),
+            pl.BlockSpec(memory_space=pltpu.VMEM),
             pl.BlockSpec((1, MODES * MODES, 8, LANES), lambda i: (i, 0, 0, 0)),
             pl.BlockSpec((8, LANES), lambda i: (i, 0)),
             pl.BlockSpec((LANES, PADF), lambda i: (0, 0)),
@@ -311,6 +332,7 @@
             pltpu.VMEM((folds * 2 * PADF, 8 * LANES), jnp.bfloat16),
             pltpu.VMEM((folds * 2 * PADF, BINS), jnp.float32),
         ],
+        compiler_params=pltpu.CompilerParams(vmem_limit_bytes=44 << 20),
         name="project",
     )(received, matrix, target, minv, jac)
 
@@ -326,8 +348,7 @@
     received = lax.all_to_all(outgoing, axes, split_axis=0, concat_axis=0, tiled=True)
     received = received.reshape(devices * HALF, LANES)
     matrix = moment_matrix(old_points, new_points, weights)
-    target, jac = index_tables(send_order[0], new_index, jacobian)
-    minv = jnp.pad(jnp.kron(jnp.eye(VARS, dtype=jnp.float32), minv_ref), ((0, 28), (0, 4)))
+    target, jac, minv = index_tables(send_order[0], new_index, jacobian, minv_ref)
     leaving = project(received, matrix, target, minv, jac.reshape(1, -1))
     leaving = leaving.reshape(devices, -1, LANES)
     arrived = lax.all_to_all(leaving, axes, split_axis=0, concat_axis=0, tiled=True)

time: 123 us -> 109 us (0.89)
  Pallas kernels: 70 us -> 59.8 us
  waiting for transfers between devices: 0.01 us -> 6.36 us
  blocking collectives: 28.9 us -> 23.4 us
  local copies, waits for them, and re-layouts: 11.3 us -> 7.88 us
    all_to_all x1, waiting for transfers between devices: 0.01 us -> 6.36 us  [local(): lax.all_to_all(outgoing, axes, split_axis=0, concat_axis=0, tiled=True)]
    all_to_all x1, blocking collectives: 28.9 us -> 23.4 us  [local(): lax.all_to_all(leaving, axes, split_axis=0, concat_axis=0, tiled=True)]
    pallas_call x1, Pallas kernels: 30.8 us -> 26.7 us  [moment_matrix(): pl.pallas_call(moment_kernel, grid=(blocks,), out_shape=jax.ShapeDtypeStr...]
    pallas_call x2, Pallas kernels: 21.2 us -> 17.3 us  [the longest x1 12.7 us: gather(): pl.pallas_call(gather_kernel, grid=(steps,), out_shape=jax.ShapeDtypeStru...]
    pallas_call x1, Pallas kernels: 18 us -> 15.8 us  [project(): pl.pallas_call(project_kernel, grid=(blocks,), out_shape=jax.ShapeDtypeSt...]
    unnamed x10 -> x12, local copies, waits for them, and re-layouts: 7.7 us -> 6.03 us
  transfers between devices with their start and end apart: 1 -> 1, of which waited for: 0 -> 1; matrix products, arithmetic and copies ran while one was open for 6% -> 5% of each run, Pallas kernels for 29% -> 29%
where the time goes in v2:
time: 109 us
  Pallas kernels  59.8 us (55%)
  blocking collectives  23.4 us (21%)
  starting transfers between devices  11.5 us (11%)
  local copies, waits for them, and re-layouts  7.88 us (7%)
  waiting for transfers between devices  6.36 us (6%)
    pallas_call x1, Pallas kernels, moment_matrix(): pl.pallas_call(moment_kernel, grid=(blocks,), out_shape=jax.ShapeDtypeStr...  26.7 us
    all_to_all x1, blocking collectives, local(): lax.all_to_all(leaving, axes, split_axis=0, concat_axis=0, tiled=True)  23.4 us
    pallas_call x1, Pallas kernels, project(): pl.pallas_call(project_kernel, grid=(blocks,), out_shape=jax.ShapeDtypeSt...  15.8 us
    pallas_call x1, Pallas kernels, gather(): pl.pallas_call(gather_kernel, grid=(steps,), out_shape=jax.ShapeDtypeStru...  12.7 us
    all_to_all x1, starting transfers between devices, local(): lax.all_to_all(outgoing, axes, split_axis=0, concat_axis=0, tiled=True)  11.5 us
    all_to_all x1, waiting for transfers between devices, local(): lax.all_to_all(outgoing, axes, split_axis=0, concat_axis=0, tiled=True)  6.36 us
    unnamed x12, local copies, waits for them, and re-layouts  6.03 us
    pallas_call x1, Pallas kernels, index_tables(): pl.pallas_call(index_kernel, out_shape=(jax.ShapeDtypeStruct((slots // LA...  4.6 us
  transfers between devices with their start and end apart: 1, of which 1 were waited for; matrix products, arithmetic and copies ran while one was open for 5% of the time, Pallas kernels for 29%

profile of v2, /device:TPU:1, one launch (start us, length us, event | category | flops | bytes accessed | tf_op | source)
XLA Modules:
  0.0 108.9 jit_solution(16282385450347245989)
XLA Ops:
  0.0 0.0 copy-start
  0.0 0.8 copy-done
  0.8 0.5 dynamic-slice_bitcast_fusion.cnt_ref
  1.4 12.7 %gather.1 = f32[6400,128]{1,0:T(8,128)} custom-call(s32[8192]{0:T(1024)} %idx_ref.1, s32[128]{0:T(128)} %dynamic-slice_bitcast_fusion.cnt_ref, f32[100,4096]{1,0:T(8,128)} %coef_ref.1), custom_call_target="tpu_custom_call" | custom-call | tf_op jit(solution)/shard_map/gather/pallas_call | solution.py:64
  14.0 11.5 %all-to-all-start = ((f32[128,25,2,128]{3,2,1,0:T(2,128)}), f32[128,25,2,128]{3,2,1,0:T(2,128)S(1)}, u32[]{:S(2)}, u32[]{:S(2)}) async-start(f32[128,25,2,128]{3,2,1,0:T(2,128)} %bitcast.23), calls=%async_computation | async-start | bytes 6553600 | tf_op jit(solution)/shard_map/all_to_all | solution.py:348
  25.5 0.0 copy-start.4
  25.5 3.6 %copy.13 = f32[1,3,1536,128]{3,2,1,0:T(8,128)} copy(f32[1,3,1536,128]{3,1,2,0:T(4,128)} %bitcast.25) | data formatting | bytes 4718592
  29.2 0.0 copy-done.4
  29.2 1.5 %copy.14 = f32[1,3,1536,128]{3,2,1,0:T(8,128)} copy(f32[1,3,1536,128]{3,1,2,0:T(4,128)S(1)} %bitcast.26) | data formatting | bytes 4718592
  30.7 4.6 %index_tables.1 = (s32[64,128]{1,0:T(8,128)}, f32[16,128]{1,0:T(8,128)}, f32[128,104]{1,0:T(8,128)}) custom-call(s32[2048]{0:T(1024)} %bitcast.31, s32[64,128]{1,0:T(8,128)} %bitcast.30, f32[16,128]{1,0:T(8,128)} %bitcast.33, s32[16,128]{1,0:T(8,128)} %bitcast.32, f32[20,20]{1,0:T(8,128)} %minv_ref.1), custom_call_target="tpu_custom_call" | custom-call | flops 4400000000 | bytes 8388608 | tf_op jit(solution)/shard_map/index_tables/pallas_call | solution.py:204
  35.3 0.0 copy-start.1
  35.3 0.0 copy-start.2
  35.3 0.0 copy-start.3
  35.3 26.7 %moment_matrix.1.m_ref = f32[8,400,8,128]{3,2,1,0:T(8,128)} custom-call(f32[3,24,64,128]{3,2,1,0:T(8,128)} %bitcast.27, f32[3,24,64,128]{3,2,1,0:T(8,128)} %bitcast.28, f32[24,64,128]{2,1,0:T(8,128)} %bitcast.29), custom_call_target="tpu_custom_call" | custom-call | flops 22000001024 | bytes 41943040 | tf_op jit(solution)/shard_map/moment_matrix/pallas_call | solution.py:147
  62.0 6.4 %all-to-all-done = f32[128,25,2,128]{3,2,1,0:T(2,128)S(1)} async-done(((f32[128,25,2,128]{3,2,1,0:T(2,128)}), f32[128,25,2,128]{3,2,1,0:T(2,128)S(1)}, u32[]{:S(2)}, u32[]{:S(2)}) %all-to-all-start) | async-done | bytes 3276832 | tf_op jit(solution)/shard_map/all_to_all | solution.py:348
  68.4 0.0 copy-done.1
  68.4 0.0 copy-done.2
  68.4 0.0 copy-done.3
  68.4 15.8 %project.1 = f32[2048,128]{1,0:T(8,128)S(1)} custom-call(f32[6400,128]{1,0:T(8,128)S(1)} %bitcast.20, f32[8,400,8,128]{3,2,1,0:T(8,128)} %moment_matrix.1.m_ref, s32[64,128]{1,0:T(8,128)S(1)} %copy-done.2, f32[128,104]{1,0:T(8,128)S(1)} %copy-done.1, f32[1,2048]{1,0:T(1,128)S(1)} %bitcast.22), custom_call_target="tpu_custom_call" | custom-call | tf_op jit(solution)/shard_map/project/pallas_call | solution.py:317
  84.2 23.4 %all_to_all.10 = f32[128,16,128]{2,1,0:T(8,128)S(1)} all-to-all(f32[128,16,128]{2,1,0:T(8,128)S(1)} %bitcast.21), channel_id=1, replica_groups=mesh['dom'=16,'sub'=8] {'dom','sub'}, dimensions={0} | all-to-all | bytes 2097152 | tf_op jit(solution)/shard_map/all_to_all | solution.py:354
  107.6 0.1 slice_bitcast_fusion
  107.7 1.3 %copy.12 = f32[100,2048]{1,0:T(8,128)} copy(f32[100,2048]{0,1:T(8,128)S(1)} %slice_bitcast_fusion) | data formatting | bytes 1638400 | tf_op jit(solution)/shard_map/transpose | solution.py:355
Async XLA Ops:
  0.0 0.8 copy-start
  14.0 54.3 %all-to-all-start = ((f32[128,25,2,128]{3,2,1,0:T(2,128)}), f32[128,25,2,128]{3,2,1,0:T(2,128)S(1)}, u32[]{:S(2)}, u32[]{:S(2)}) async-start(f32[128,25,2,128]{3,2,1,0:T(2,128)} %bitcast.23), calls=%async_computation | async-start | bytes 6553600 | tf_op jit(solution)/shard_map/all_to_all | solution.py:348
  25.5 3.6 %copy-start.4 = (f32[3,196608]{1,0:T(4,128)S(1)}, f32[3,196608]{1,0:T(4,128)}, u32[]{:S(2)}) copy-start(f32[3,196608]{1,0:T(4,128)} %param.15) | copy-start | bytes 7077892
  35.3 33.1 %copy-start.1 = (f32[128,104]{1,0:T(8,128)S(1)}, f32[128,104]{1,0:T(8,128)}, u32[]{:S(2)}) copy-start(f32[128,104]{1,0:T(8,128)} %get-tuple-element.9.minv_ref) | copy-start | bytes 159748
  35.3 33.1 %copy-start.2 = (s32[64,128]{1,0:T(8,128)S(1)}, s32[64,128]{1,0:T(8,128)}, u32[]{:S(2)}) copy-start(s32[64,128]{1,0:T(8,128)} %get-tuple-element.8.target_ref) | copy-start | bytes 98308
  35.3 33.1 %copy-start.3 = (f32[16,128]{1,0:T(8,128)S(1)}, f32[16,128]{1,0:T(8,128)}, u32[]{:S(2)}) copy-start(f32[16,128]{1,0:T(8,128)} %get-tuple-element.10) | copy-start | bytes 24580

commit v3 on v2

--- a/solution.py
+++ b/solution.py
@@ -15,8 +15,9 @@
 LANES = 128
 
 
-def gather_kernel(idx_ref, cnt_ref, coef_ref, out_ref, tab_ref, buf_ref):
+def gather_kernel(subs, idx_ref, cnt_ref, coef_ref, out_ref, tab_ref, buf_ref):
     part = pl.program_id(0)
+    myself = lax.axis_index("dom") * subs + lax.axis_index("sub")
     width = coef_ref.shape[1]
     pairs = buf_ref.shape[0] // LANES
     lane = lax.broadcasted_iota(jnp.int32, (1, LANES), 1)
@@ -47,7 +48,7 @@
     turned = [buf_ref[u * LANES : (u + 1) * LANES, :].T for u in range(pairs)]
     for u in range(pairs):
         pair = part * pairs + u
-        limit = jnp.where(low, cnt_ref[2 * pair], cnt_ref[2 * pair + 1] + 64)
+        limit = jnp.where(low, cnt_ref[myself, 2 * pair], cnt_ref[myself, 2 * pair + 1] + 64)
         live = lane < limit
         first = jnp.where(live, turned[u][:HALF], 0.0)
         second = jnp.where(live, turned[u][64 : 64 + HALF], 0.0)
@@ -57,12 +58,12 @@
         )
 
 
-def gather(old_coef, old_index, counts, steps=4):
+def gather(old_coef, old_index, pair_count, subs, steps=4):
     slots = old_index.shape[0]
     rows, width = old_coef.shape
     total = slots // CAP * HALF
     return pl.pallas_call(
-        gather_kernel,
+        functools.partial(gather_kernel, subs),
         grid=(steps,),
         out_shape=jax.ShapeDtypeStruct((total, LANES), jnp.float32),
         in_specs=[
@@ -76,7 +77,7 @@
             pltpu.VMEM((slots // steps, LANES), jnp.float32),
         ],
         name="gather",
-    )(old_index, counts, old_coef)
+    )(old_index, pair_count, old_coef)
 
 
 def monomials(first, second, third):
@@ -213,6 +214,7 @@
         cost_estimate=pl.CostEstimate(
             flops=int(4e-6 * 1.1e15), bytes_accessed=8 * 2**20, transcendentals=0
         ),
+        compiler_params=pltpu.CompilerParams(vmem_limit_bytes=8 << 20),
         name="index_tables",
     )(
         order,
@@ -341,14 +343,13 @@
           minv_ref, send_order):
     axes = ("dom", "sub")
     devices = lax.axis_size(axes)
-    myself = lax.axis_index(axes)
-    counts = lax.dynamic_slice_in_dim(pair_count, myself, 1, 0)[0]
-    outgoing = gather(old_coef, old_index, counts)
+    outgoing = gather(old_coef, old_index, pair_count, lax.axis_size("sub"))
     outgoing = outgoing.reshape(devices, HALF // 2, 2, LANES)
     received = lax.all_to_all(outgoing, axes, split_axis=0, concat_axis=0, tiled=True)
     received = received.reshape(devices * HALF, LANES)
+    target, jac, minv = index_tables(send_order[0], new_index, jacobian, minv_ref)
+    old_points, new_points, target = lax.optimization_barrier((old_points, new_points, target))
     matrix = moment_matrix(old_points, new_points, weights)
-    target, jac, minv = index_tables(send_order[0], new_index, jacobian, minv_ref)
     leaving = project(received, matrix, target, minv, jac.reshape(1, -1))
     leaving = leaving.reshape(devices, -1, LANES)
     arrived = lax.all_to_all(leaving, axes, split_axis=0, concat_axis=0, tiled=True)

time: 109 us -> 109 us (level)
  local copies, waits for them, and re-layouts: 7.88 us -> 5.65 us
  waiting for transfers between devices: 6.36 us -> 8.26 us
    all_to_all x1, waiting for transfers between devices: 6.36 us -> 8.26 us  [local(): lax.all_to_all(outgoing, axes, split_axis=0, concat_axis=0, tiled=True)]
    unnamed x12 -> x14, local copies, waits for them, and re-layouts: 6.03 us -> 4.31 us
  transfers between devices with their start and end apart: 1 -> 1, of which waited for: 1 -> 1; matrix products, arithmetic and copies ran while one was open for 5% -> 3% of each run, Pallas kernels for 29% -> 28%
where the time goes in v3:
time: 109 us; the launch traced here: 108 us
  Pallas kernels  59.5 us (55%)
  blocking collectives  23.4 us (21%)
  starting transfers between devices  11.5 us (11%)
  waiting for transfers between devices  8.26 us (8%)
  local copies, waits for them, and re-layouts  5.65 us (5%)
    pallas_call x1, Pallas kernels, moment_matrix(): pl.pallas_call(moment_kernel, grid=(blocks,), out_shape=jax.ShapeDtypeStr...  26.6 us
    all_to_all x1, blocking collectives, local(): lax.all_to_all(leaving, axes, split_axis=0, concat_axis=0, tiled=True)  23.4 us
    pallas_call x1, Pallas kernels, project(): pl.pallas_call(project_kernel, grid=(blocks,), out_shape=jax.ShapeDtypeSt...  15.8 us
    pallas_call x1, Pallas kernels, gather(): pl.pallas_call(functools.partial(gather_kernel, subs), grid=(steps,), out...  13.5 us
    all_to_all x1, starting transfers between devices, local(): lax.all_to_all(outgoing, axes, split_axis=0, concat_axis=0, tiled=True)  11.5 us
    all_to_all x1, waiting for transfers between devices, local(): lax.all_to_all(outgoing, axes, split_axis=0, concat_axis=0, tiled=True)  8.26 us
    unnamed x14, local copies, waits for them, and re-layouts  4.31 us
    pallas_call x1, Pallas kernels, index_tables(): pl.pallas_call(index_kernel, out_shape=(jax.ShapeDtypeStruct((slots // LA...  3.57 us
  transfers between devices with their start and end apart: 1, of which 1 were waited for; matrix products, arithmetic and copies ran while one was open for 3% of the time, Pallas kernels for 28%

profile of v3, /device:TPU:1, one launch (start us, length us, event | category | flops | bytes accessed | tf_op | source)
XLA Modules:
  0.0 108.4 jit_solution(10150627288638584835)
XLA Ops:
  0.0 13.5 %gather.1 = f32[6400,128]{1,0:T(8,128)} custom-call(s32[8192]{0:T(1024)} %idx_ref.1, s32[128,128]{1,0:T(8,128)} %cnt_ref.1, f32[100,4096]{1,0:T(8,128)} %coef_ref.1), custom_call_target="tpu_custom_call" | custom-call | tf_op jit(solution)/shard_map/gather/pallas_call | solution.py:65
  13.5 0.0 copy-start
  13.5 0.0 copy-start.1
  13.5 0.0 copy-start.2
  13.5 0.0 copy-start.3
  13.5 11.5 %all-to-all-start = ((f32[128,25,2,128]{3,2,1,0:T(2,128)}), f32[128,25,2,128]{3,2,1,0:T(2,128)S(1)}, u32[]{:S(2)}, u32[]{:S(2)}) async-start(f32[128,25,2,128]{3,2,1,0:T(2,128)} %bitcast.25), calls=%async_computation | async-start | bytes 6553600 | tf_op jit(solution)/shard_map/all_to_all | solution.py:348
  25.1 0.0 copy-done
  25.1 0.0 copy-done.1
  25.1 0.0 copy-done.2
  25.1 0.0 copy-done.3
  25.1 0.0 copy-start.4
  25.1 3.6 %index_tables.1 = (s32[64,128]{1,0:T(8,128)S(1)}, f32[16,128]{1,0:T(8,128)S(1)}, f32[128,104]{1,0:T(8,128)S(1)}) custom-call(s32[2048]{0:T(1024)S(1)} %bitcast.22, s32[64,128]{1,0:T(8,128)S(1)} %bitcast.21, f32[16,128]{1,0:T(8,128)S(1)} %bitcast.24, s32[16,128]{1,0:T(8,128)S(1)} %bitcast.23, f32[20,20]{1,0:T(8,128)S(1)} %copy-done.1), custom_call_target="tpu_custom_call" | custom-call | flops 4400000000 | bytes 8388608 | tf_op jit(solution)/shard_map/index_tables/pallas_call | solution.py:205
  28.7 0.0 copy-start.5
  28.7 0.0 copy-done.4
  28.7 1.6 %copy.13 = f32[1,3,1536,128]{3,2,1,0:T(8,128)} copy(f32[1,3,1536,128]{3,1,2,0:T(4,128)S(1)} %bitcast.27) | data formatting | bytes 4718592
  30.3 1.1 %copy-done.5 = f32[3,196608]{1,0:T(4,128)S(1)} copy-done((f32[3,196608]{1,0:T(4,128)S(1)}, f32[3,196608]{1,0:T(4,128)}, u32[]{:S(2)}) %copy-start.5) | copy-done | bytes 2359320
  31.4 1.6 %copy.14 = f32[1,3,1536,128]{3,2,1,0:T(8,128)} copy(f32[1,3,1536,128]{3,1,2,0:T(4,128)S(1)} %bitcast.28) | data formatting | bytes 4718592
  33.0 26.6 %moment_matrix.1.m_ref = f32[8,400,8,128]{3,2,1,0:T(8,128)} custom-call(f32[3,24,64,128]{3,2,1,0:T(8,128)} %bitcast.29, f32[3,24,64,128]{3,2,1,0:T(8,128)} %bitcast.30, f32[24,64,128]{2,1,0:T(8,128)} %bitcast.31), custom_call_target="tpu_custom_call" | custom-call | flops 22000001024 | bytes 41943040 | tf_op jit(solution)/shard_map/moment_matrix/pallas_call | solution.py:148
  59.6 8.3 %all-to-all-done = f32[128,25,2,128]{3,2,1,0:T(2,128)S(1)} async-done(((f32[128,25,2,128]{3,2,1,0:T(2,128)}), f32[128,25,2,128]{3,2,1,0:T(2,128)S(1)}, u32[]{:S(2)}, u32[]{:S(2)}) %all-to-all-start) | async-done | bytes 3276832 | tf_op jit(solution)/shard_map/all_to_all | solution.py:348
  67.9 15.8 %project.1 = f32[2048,128]{1,0:T(8,128)S(1)} custom-call(f32[6400,128]{1,0:T(8,128)S(1)} %bitcast.18, f32[8,400,8,128]{3,2,1,0:T(8,128)} %moment_matrix.1.m_ref, s32[64,128]{1,0:T(8,128)S(1)} %get-tuple-element.14.target_ref, f32[128,104]{1,0:T(8,128)S(1)} %get-tuple-element.15.minv_ref, f32[1,2048]{1,0:T(1,128)S(1)} %bitcast.20), custom_call_target="tpu_custom_call" | custom-call | tf_op jit(solution)/shard_map/project/pallas_call | solution.py:319
  83.7 23.4 %all_to_all.10 = f32[128,16,128]{2,1,0:T(8,128)S(1)} all-to-all(f32[128,16,128]{2,1,0:T(8,128)S(1)} %bitcast.19), channel_id=1, replica_groups=mesh['dom'=16,'sub'=8] {'dom','sub'}, dimensions={0} | all-to-all | bytes 2097152 | tf_op jit(solution)/shard_map/all_to_all | solution.py:355
  107.1 0.1 slice_bitcast_fusion
  107.2 1.3 %copy.12 = f32[100,2048]{1,0:T(8,128)} copy(f32[100,2048]{0,1:T(8,128)S(1)} %slice_bitcast_fusion) | data formatting | bytes 1638400 | tf_op jit(solution)/shard_map/transpose | solution.py:356
Async XLA Ops:
  13.5 11.5 %copy-start = (s32[8192]{0:T(1024)S(1)}, s32[8192]{0:T(1024)}, u32[]{:S(2)}) copy-start(s32[8192]{0:T(1024)} %param.13) | copy-start | bytes 98308
  13.5 11.5 %copy-start.1 = (f32[20,20]{1,0:T(8,128)S(1)}, f32[20,20]{1,0:T(8,128)}, u32[]{:S(2)}) copy-start(f32[20,20]{1,0:T(8,128)} %minv_ref.1) | copy-start | bytes 4804
  13.5 11.5 %copy-start.2 = (s32[1,2048]{1,0:T(1,128)S(1)}, s32[1,2048]{1,0:T(1,128)}, u32[]{:S(2)}) copy-start(s32[1,2048]{1,0:T(1,128)} %param.19) | copy-start | bytes 24580
  13.5 11.6 %copy-start.3 = (f32[2048]{0:T(1024)S(1)}, f32[2048]{0:T(1024)}, u32[]{:S(2)}) copy-start(f32[2048]{0:T(1024)} %param.17) | copy-start | bytes 24580
  13.5 54.3 %all-to-all-start = ((f32[128,25,2,128]{3,2,1,0:T(2,128)}), f32[128,25,2,128]{3,2,1,0:T(2,128)S(1)}, u32[]{:S(2)}, u32[]{:S(2)}) async-start(f32[128,25,2,128]{3,2,1,0:T(2,128)} %bitcast.25), calls=%async_computation | async-start | bytes 6553600 | tf_op jit(solution)/shard_map/all_to_all | solution.py:348
  25.1 3.6 %copy-start.4 = (f32[3,196608]{1,0:T(4,128)S(1)}, f32[3,196608]{1,0:T(4,128)}, u32[]{:S(2)}) copy-start(f32[3,196608]{1,0:T(4,128)} %param.14) | copy-start | bytes 7077892
  28.7 2.7 %copy-start.5 = (f32[3,196608]{1,0:T(4,128)S(1)}, f32[3,196608]{1,0:T(4,128)}, u32[]{:S(2)}) copy-start(f32[3,196608]{1,0:T(4,128)} %param.15) | copy-start | bytes 7077892

commit v4 on v3

--- a/solution.py
+++ b/solution.py
@@ -15,9 +15,12 @@
 LANES = 128
 
 
-def gather_kernel(subs, idx_ref, cnt_ref, coef_ref, out_ref, tab_ref, buf_ref):
+def gather_kernel(
+    subs, idx_hbm, cnt_hbm, coef_hbm, out_ref, tab_ref, buf_ref, coef_ref, idx_ref, cnt_ref, sems
+):
     part = pl.program_id(0)
-    myself = lax.axis_index("dom") * subs + lax.axis_index("sub")
+    rank = lax.axis_index("dom") * subs + lax.axis_index("sub")
+    myself = rank % 8
     width = coef_ref.shape[1]
     pairs = buf_ref.shape[0] // LANES
     lane = lax.broadcasted_iota(jnp.int32, (1, LANES), 1)
@@ -25,6 +28,23 @@
 
     @pl.when(part == 0)
     def _():
+        cuts = 4
+        span = width // cuts
+        wide = [
+            pltpu.make_async_copy(
+                coef_hbm.at[:, pl.ds(c * span, span)],
+                coef_ref.at[:, pl.ds(c * span, span)],
+                sems.at[c],
+            )
+            for c in range(cuts)
+        ]
+        start = pl.multiple_of(rank - myself, 8)
+        small = [
+            pltpu.make_async_copy(idx_hbm, idx_ref, sems.at[cuts]),
+            pltpu.make_async_copy(cnt_hbm.at[pl.ds(start, 8), :], cnt_ref, sems.at[cuts + 1]),
+        ]
+        for copy in wide[:1] + small + wide[1:]:
+            copy.start()
         pad = jnp.zeros((64 - HALF, LANES), jnp.float32)
 
         def build(j, carry):
@@ -34,7 +54,11 @@
             tab_ref[pl.ds(start, LANES), :] = wide.T
             return carry
 
-        lax.fori_loop(0, width // LANES, build, 0, unroll=4)
+        for c in range(cuts):
+            wide[c].wait()
+            lax.fori_loop(c * (span // LANES), (c + 1) * (span // LANES), build, 0, unroll=4)
+        for copy in small:
+            copy.wait()
 
     def fetch(t, carry):
         base = pl.multiple_of(t * LANES, LANES)
@@ -66,15 +90,15 @@
         functools.partial(gather_kernel, subs),
         grid=(steps,),
         out_shape=jax.ShapeDtypeStruct((total, LANES), jnp.float32),
-        in_specs=[
-            pl.BlockSpec(memory_space=pltpu.SMEM),
-            pl.BlockSpec(memory_space=pltpu.SMEM),
-            pl.BlockSpec((rows, width), lambda i: (0, 0), pipeline_mode=pl.Buffered(1)),
-        ],
+        in_specs=[pl.BlockSpec(memory_space=pl.ANY)] * 3,
         out_specs=pl.BlockSpec((total // steps, LANES), lambda i: (i, 0)),
         scratch_shapes=[
             pltpu.VMEM((width, LANES), jnp.float32),
             pltpu.VMEM((slots // steps, LANES), jnp.float32),
+            pltpu.VMEM((rows, width), jnp.float32),
+            pltpu.SMEM((slots,), jnp.int32),
+            pltpu.SMEM((8, pair_count.shape[1]), jnp.int32),
+            pltpu.SemaphoreType.DMA((6,)),
         ],
         name="gather",
     )(old_index, pair_count, old_coef)

time: 109 us -> 108 us (level)
  Pallas kernels: 59.5 us -> 58.3 us
    pallas_call x1, Pallas kernels: 13.5 us -> 12.3 us  [gather(): pl.pallas_call(functools.partial(gather_kernel, subs), grid=(steps,), out...]
where the time goes in v4:
time: 108 us; the launch traced here: 107 us
  Pallas kernels  58.3 us (54%)
  blocking collectives  23.4 us (22%)
  starting transfers between devices  11.5 us (11%)
  waiting for transfers between devices  8.26 us (8%)
  local copies, waits for them, and re-layouts  5.65 us (5%)
    pallas_call x1, Pallas kernels, moment_matrix(): pl.pallas_call(moment_kernel, grid=(blocks,), out_shape=jax.ShapeDtypeStr...  26.6 us
    all_to_all x1, blocking collectives, local(): lax.all_to_all(leaving, axes, split_axis=0, concat_axis=0, tiled=True)  23.4 us
    pallas_call x1, Pallas kernels, project(): pl.pallas_call(project_kernel, grid=(blocks,), out_shape=jax.ShapeDtypeSt...  15.8 us
    pallas_call x1, Pallas kernels, gather(): pl.pallas_call(functools.partial(gather_kernel, subs), grid=(steps,), out...  12.3 us
    all_to_all x1, starting transfers between devices, local(): lax.all_to_all(outgoing, axes, split_axis=0, concat_axis=0, tiled=True)  11.5 us
    all_to_all x1, waiting for transfers between devices, local(): lax.all_to_all(outgoing, axes, split_axis=0, concat_axis=0, tiled=True)  8.26 us
    unnamed x14, local copies, waits for them, and re-layouts  4.32 us
    pallas_call x1, Pallas kernels, index_tables(): pl.pallas_call(index_kernel, out_shape=(jax.ShapeDtypeStruct((slots // LA...  3.57 us
  transfers between devices with their start and end apart: 1, of which 1 were waited for; matrix products, arithmetic and copies ran while one was open for 3% of the time, Pallas kernels for 28%

profile of v4, /device:TPU:1, one launch (start us, length us, event | category | flops | bytes accessed | tf_op | source)
XLA Modules:
  0.0 107.3 jit_solution(11865915867412624317)
XLA Ops:
  0.0 12.3 %gather.1 = f32[6400,128]{1,0:T(8,128)} custom-call(s32[8192]{0:T(1024)} %idx_hbm.1, s32[128,128]{1,0:T(8,128)} %cnt_hbm.1, f32[100,4096]{1,0:T(8,128)} %coef_hbm.1), custom_call_target="tpu_custom_call" | custom-call | tf_op jit(solution)/shard_map/gather/pallas_call | solution.py:89
  12.3 0.0 copy-start
  12.3 0.0 copy-start.1
  12.3 0.0 copy-start.2
  12.3 0.0 copy-start.3
  12.3 11.5 %all-to-all-start = ((f32[128,25,2,128]{3,2,1,0:T(2,128)}), f32[128,25,2,128]{3,2,1,0:T(2,128)S(1)}, u32[]{:S(2)}, u32[]{:S(2)}) async-start(f32[128,25,2,128]{3,2,1,0:T(2,128)} %bitcast.25), calls=%async_computation | async-start | bytes 6553600 | tf_op jit(solution)/shard_map/all_to_all | solution.py:372
  23.9 0.0 copy-done
  23.9 0.0 copy-done.1
  23.9 0.0 copy-done.2
  23.9 0.0 copy-done.3
  23.9 0.0 copy-start.4
  23.9 3.6 %index_tables.1 = (s32[64,128]{1,0:T(8,128)S(1)}, f32[16,128]{1,0:T(8,128)S(1)}, f32[128,104]{1,0:T(8,128)S(1)}) custom-call(s32[2048]{0:T(1024)S(1)} %bitcast.22, s32[64,128]{1,0:T(8,128)S(1)} %bitcast.21, f32[16,128]{1,0:T(8,128)S(1)} %bitcast.24, s32[16,128]{1,0:T(8,128)S(1)} %bitcast.23, f32[20,20]{1,0:T(8,128)S(1)} %copy-done.1), custom_call_target="tpu_custom_call" | custom-call | flops 4400000000 | bytes 8388608 | tf_op jit(solution)/shard_map/index_tables/pallas_call | solution.py:229
  27.5 0.0 copy-start.5
  27.5 0.0 copy-done.4
  27.5 1.6 %copy.13 = f32[1,3,1536,128]{3,2,1,0:T(8,128)} copy(f32[1,3,1536,128]{3,1,2,0:T(4,128)S(1)} %bitcast.27) | data formatting | bytes 4718592
  29.1 1.1 %copy-done.5 = f32[3,196608]{1,0:T(4,128)S(1)} copy-done((f32[3,196608]{1,0:T(4,128)S(1)}, f32[3,196608]{1,0:T(4,128)}, u32[]{:S(2)}) %copy-start.5) | copy-done | bytes 2359320
  30.2 1.6 %copy.14 = f32[1,3,1536,128]{3,2,1,0:T(8,128)} copy(f32[1,3,1536,128]{3,1,2,0:T(4,128)S(1)} %bitcast.28) | data formatting | bytes 4718592
  31.8 26.6 %moment_matrix.1.m_ref = f32[8,400,8,128]{3,2,1,0:T(8,128)} custom-call(f32[3,24,64,128]{3,2,1,0:T(8,128)} %bitcast.29, f32[3,24,64,128]{3,2,1,0:T(8,128)} %bitcast.30, f32[24,64,128]{2,1,0:T(8,128)} %bitcast.31), custom_call_target="tpu_custom_call" | custom-call | flops 22000001024 | bytes 41943040 | tf_op jit(solution)/shard_map/moment_matrix/pallas_call | solution.py:172
  58.4 8.3 %all-to-all-done = f32[128,25,2,128]{3,2,1,0:T(2,128)S(1)} async-done(((f32[128,25,2,128]{3,2,1,0:T(2,128)}), f32[128,25,2,128]{3,2,1,0:T(2,128)S(1)}, u32[]{:S(2)}, u32[]{:S(2)}) %all-to-all-start) | async-done | bytes 3276832 | tf_op jit(solution)/shard_map/all_to_all | solution.py:372
  66.7 15.8 %project.1 = f32[2048,128]{1,0:T(8,128)S(1)} custom-call(f32[6400,128]{1,0:T(8,128)S(1)} %bitcast.18, f32[8,400,8,128]{3,2,1,0:T(8,128)} %moment_matrix.1.m_ref, s32[64,128]{1,0:T(8,128)S(1)} %get-tuple-element.14.target_ref, f32[128,104]{1,0:T(8,128)S(1)} %get-tuple-element.15.minv_ref, f32[1,2048]{1,0:T(1,128)S(1)} %bitcast.20), custom_call_target="tpu_custom_call" | custom-call | tf_op jit(solution)/shard_map/project/pallas_call | solution.py:343
  82.5 23.4 %all_to_all.10 = f32[128,16,128]{2,1,0:T(8,128)S(1)} all-to-all(f32[128,16,128]{2,1,0:T(8,128)S(1)} %bitcast.19), channel_id=1, replica_groups=mesh['dom'=16,'sub'=8] {'dom','sub'}, dimensions={0} | all-to-all | bytes 2097152 | tf_op jit(solution)/shard_map/all_to_all | solution.py:379
  105.9 0.1 slice_bitcast_fusion
  106.0 1.3 %copy.12 = f32[100,2048]{1,0:T(8,128)} copy(f32[100,2048]{0,1:T(8,128)S(1)} %slice_bitcast_fusion) | data formatting | bytes 1638400 | tf_op jit(solution)/shard_map/transpose | solution.py:380
Async XLA Ops:
  12.3 11.6 %copy-start = (s32[8192]{0:T(1024)S(1)}, s32[8192]{0:T(1024)}, u32[]{:S(2)}) copy-start(s32[8192]{0:T(1024)} %param.13) | copy-start | bytes 98308
  12.3 11.6 %copy-start.1 = (f32[20,20]{1,0:T(8,128)S(1)}, f32[20,20]{1,0:T(8,128)}, u32[]{:S(2)}) copy-start(f32[20,20]{1,0:T(8,128)} %minv_ref.1) | copy-start | bytes 4804
  12.3 11.6 %copy-start.2 = (s32[1,2048]{1,0:T(1,128)S(1)}, s32[1,2048]{1,0:T(1,128)}, u32[]{:S(2)}) copy-start(s32[1,2048]{1,0:T(1,128)} %param.19) | copy-start | bytes 24580
  12.3 11.6 %copy-start.3 = (f32[2048]{0:T(1024)S(1)}, f32[2048]{0:T(1024)}, u32[]{:S(2)}) copy-start(f32[2048]{0:T(1024)} %param.17) | copy-start | bytes 24580
  12.3 54.3 %all-to-all-start = ((f32[128,25,2,128]{3,2,1,0:T(2,128)}), f32[128,25,2,128]{3,2,1,0:T(2,128)S(1)}, u32[]{:S(2)}, u32[]{:S(2)}) async-start(f32[128,25,2,128]{3,2,1,0:T(2,128)} %bitcast.25), calls=%async_computation | async-start | bytes 6553600 | tf_op jit(solution)/shard_map/all_to_all | solution.py:372
  23.9 3.6 %copy-start.4 = (f32[3,196608]{1,0:T(4,128)S(1)}, f32[3,196608]{1,0:T(4,128)}, u32[]{:S(2)}) copy-start(f32[3,196608]{1,0:T(4,128)} %param.14) | copy-start | bytes 7077892
  27.5 2.7 %copy-start.5 = (f32[3,196608]{1,0:T(4,128)S(1)}, f32[3,196608]{1,0:T(4,128)}, u32[]{:S(2)}) copy-start(f32[3,196608]{1,0:T(4,128)} %param.15) | copy-start | bytes 7077892

commit v5 on v4

--- a/solution.py
+++ b/solution.py
@@ -192,8 +192,13 @@
 
 def index_kernel(order_s, index_ref, jac_ref, order_ref, minv_ref, target_ref, jacp_ref, wide_ref):
     wide_ref[...] = jnp.zeros_like(wide_ref)
+    span = MODES // 2
     for v in range(VARS):
-        wide_ref[v * MODES : (v + 1) * MODES, v * MODES : (v + 1) * MODES] = minv_ref[...]
+        for h in range(2):
+            start = h * PADH + v * span
+            wide_ref[v * MODES : (v + 1) * MODES, start : start + span] = minv_ref[
+                :, h * span : (h + 1) * span
+            ]
     rows = jac_ref.shape[0]
     place = lax.broadcasted_iota(jnp.int32, (rows, LANES), 0) * LANES + lax.broadcasted_iota(
         jnp.int32, (rows, LANES), 1
@@ -231,7 +236,7 @@
         out_shape=(
             jax.ShapeDtypeStruct((slots // LANES, LANES), jnp.int32),
             jax.ShapeDtypeStruct((count // LANES, LANES), jnp.float32),
-            jax.ShapeDtypeStruct((LANES, PADF), jnp.float32),
+            jax.ShapeDtypeStruct((LANES, 2 * PADH), jnp.float32),
         ),
         in_specs=[pl.BlockSpec(memory_space=pltpu.SMEM), vm, vm, vm, vm],
         out_specs=(vm, vm, vm),
@@ -249,22 +254,22 @@
     )
 
 
-PADF = 104
+PADH = 56
 BINS = 512
 
 
 def project_kernel(
-    recv_ref, m_ref, target_ref, minv_ref, jac_ref, out_ref, coef_ref, y_ref, lhs_ref, acc_ref
+    recv_ref, m_ref, target_ref, minv_ref, jac_ref, out_ref, coef_ref, y0, y1, lhs0, lhs1, acc0, acc1
 ):
     turn = pl.program_id(0)
-    folds = acc_ref.shape[0] // (2 * PADF)
+    folds = acc0.shape[0] // (2 * PADH)
     half = jnp.bfloat16
     single = jnp.float32
 
     @pl.when(turn == 0)
     def _():
-        acc_ref[...] = jnp.zeros_like(acc_ref)
-        y_ref[...] = jnp.zeros_like(y_ref)
+        for ref in (acc0, acc1, y0, y1):
+            ref[...] = jnp.zeros_like(ref)
 
     low = lax.broadcasted_iota(jnp.int32, (8, LANES), 1) < 64
     first = pl.multiple_of(turn * (8 * ROWS), 8)
@@ -273,49 +278,61 @@
         odd = recv_ref[pl.ds(first + HALF + r, 8, stride=ROWS), :]
         coef_ref[r] = jnp.where(low, even, pltpu.roll(odd, 64, 1))
         coef_ref[r + HALF] = jnp.where(low, pltpu.roll(even, 64, 1), odd)
-    tile = 4
-    for m0 in range(0, MODES, tile):
-        accs = [None] * (tile * VARS)
-        for k in range(MODES):
-            coefs = [coef_ref[v * MODES + k] for v in range(VARS)]
-            for i in range(tile):
-                entry = m_ref[0, (m0 + i) * MODES + k]
-                for v in range(VARS):
-                    term = entry * coefs[v]
-                    old = accs[i * VARS + v]
-                    accs[i * VARS + v] = term if old is None else old + term
-        for i in range(tile):
-            for v in range(VARS):
-                f = v * MODES + m0 + i
-                y_ref[pl.ds((f // 8) * 64 + f % 8, 8, stride=8), :] = accs[i * VARS + v]
     slots = 8 * LANES
-    rows = []
-    for fb in range(PADF // 8):
-        rows.append(
-            jnp.concatenate(
-                [y_ref[(fb * 8 + g) * 8 : (fb * 8 + g) * 8 + 8, :] for g in range(8)], axis=1
-            )
-        )
-    y = jnp.concatenate(rows, axis=0)
-    high = y.astype(half).astype(single)
-    both = jnp.concatenate([high, y - high], axis=0).astype(half)
     target = jnp.concatenate([target_ref[g : g + 1, :] for g in range(8)], axis=1)
     fold = target // BINS
-    for a in range(folds):
-        keep = jnp.where(fold == a, 1.0, 0.0).astype(half)
-        lhs_ref[a * 2 * PADF : (a + 1) * 2 * PADF, :] = both * keep
     bins = lax.broadcasted_iota(jnp.int32, (256, slots), 0).astype(single).astype(half)
     within = target & (BINS - 1)
     parts = []
     for h in range(BINS // 256):
         wanted = (within - 256 * h).astype(single).astype(half)
         parts.append(jnp.where(bins == wanted, jnp.array(1, half), jnp.array(0, half)))
-    acc_ref[...] += lax.dot_general(
-        lhs_ref[...],
-        jnp.concatenate(parts, axis=0),
-        (((1,), (1,)), ((), ())),
-        preferred_element_type=single,
-    )
+    hot = jnp.concatenate(parts, axis=0)
+    tile = 5
+    span = MODES // 2
+
+    def apply(y_ref, start):
+        for m0 in range(start, start + span, tile):
+            accs = [None] * (tile * VARS)
+            for k in range(MODES):
+                coefs = [coef_ref[v * MODES + k] for v in range(VARS)]
+                for i in range(tile):
+                    entry = m_ref[0, (m0 + i) * MODES + k]
+                    for v in range(VARS):
+                        term = entry * coefs[v]
+                        old = accs[i * VARS + v]
+                        accs[i * VARS + v] = term if old is None else old + term
+            for i in range(tile):
+                for v in range(VARS):
+                    f = v * span + m0 - start + i
+                    y_ref[pl.ds((f // 8) * 64 + f % 8, 8, stride=8), :] = accs[i * VARS + v]
+
+    def widen(y_ref, lhs_ref):
+        rows = []
+        for fb in range(PADH // 8):
+            rows.append(
+                jnp.concatenate(
+                    [y_ref[(fb * 8 + g) * 8 : (fb * 8 + g) * 8 + 8, :] for g in range(8)], axis=1
+                )
+            )
+        y = jnp.concatenate(rows, axis=0)
+        high = y.astype(half).astype(single)
+        both = jnp.concatenate([high, y - high], axis=0).astype(half)
+        for a in range(folds):
+            keep = jnp.where(fold == a, 1.0, 0.0).astype(half)
+            lhs_ref[a * 2 * PADH : (a + 1) * 2 * PADH, :] = both * keep
+
+    def deposit(lhs_ref, acc_ref):
+        acc_ref[...] += lax.dot_general(
+            lhs_ref[...], hot, (((1,), (1,)), ((), ())), preferred_element_type=single
+        )
+
+    apply(y0, 0)
+    widen(y0, lhs0)
+    deposit(lhs0, acc0)
+    apply(y1, span)
+    widen(y1, lhs1)
+    deposit(lhs1, acc1)
 
     @pl.when(turn == pl.num_programs(0) - 1)
     def _():
@@ -324,8 +341,14 @@
         left = jnp.concatenate([minv_h, minv_h, minv - minv_h], axis=1).astype(half)
         scale = 1.0 / jac_ref[...]
         for a in range(folds):
-            base = a * 2 * PADF
-            rhs = acc_ref[base : base + PADF, :] + acc_ref[base + PADF : base + 2 * PADF, :]
+            base = a * 2 * PADH
+            rhs = jnp.concatenate(
+                [
+                    ref[base : base + PADH, :] + ref[base + PADH : base + 2 * PADH, :]
+                    for ref in (acc0, acc1)
+                ],
+                axis=0,
+            )
             rhs_h = rhs.astype(half).astype(single)
             right = jnp.concatenate([rhs_h, rhs - rhs_h, rhs_h], axis=0).astype(half)
             done = jnp.dot(left, right, preferred_element_type=single)
@@ -348,15 +371,18 @@
             pl.BlockSpec(memory_space=pltpu.VMEM),
             pl.BlockSpec((1, MODES * MODES, 8, LANES), lambda i: (i, 0, 0, 0)),
             pl.BlockSpec((8, LANES), lambda i: (i, 0)),
-            pl.BlockSpec((LANES, PADF), lambda i: (0, 0)),
+            pl.BlockSpec((LANES, 2 * PADH), lambda i: (0, 0)),
             pl.BlockSpec((1, count), lambda i: (0, 0)),
         ],
         out_specs=pl.BlockSpec((count, LANES), lambda i: (0, 0)),
         scratch_shapes=[
             pltpu.VMEM((ROWS, 8, LANES), jnp.float32),
-            pltpu.VMEM((PADF * 8, LANES), jnp.float32),
-            pltpu.VMEM((folds * 2 * PADF, 8 * LANES), jnp.bfloat16),
-            pltpu.VMEM((folds * 2 * PADF, BINS), jnp.float32),
+            pltpu.VMEM((PADH * 8, LANES), jnp.float32),
+            pltpu.VMEM((PADH * 8, LANES), jnp.float32),
+            pltpu.VMEM((folds * 2 * PADH, 8 * LANES), jnp.bfloat16),
+            pltpu.VMEM((folds * 2 * PADH, 8 * LANES), jnp.bfloat16),
+            pltpu.VMEM((folds * 2 * PADH, BINS), jnp.float32),
+            pltpu.VMEM((folds * 2 * PADH, BINS), jnp.float32),
         ],
         compiler_params=pltpu.CompilerParams(vmem_limit_bytes=44 << 20),
         name="project",

time: 108 us -> 106 us (0.981)
  Pallas kernels: 58.3 us -> 57.1 us
    pallas_call x1, Pallas kernels: 15.8 us -> 14.5 us  [project(): pl.pallas_call(project_kernel, grid=(blocks,), out_shape=jax.ShapeDtypeSt...]
  transfers between devices with their start and end apart: 1 -> 1, of which waited for: 1 -> 1; matrix products, arithmetic and copies ran while one was open for 3% -> 3% of each run, Pallas kernels for 28% -> 29%
where the time goes in v5:
time: 106 us
  Pallas kernels  57.1 us (54%)
  blocking collectives  23.4 us (22%)
  starting transfers between devices  11.5 us (11%)
  waiting for transfers between devices  8.24 us (8%)
  local copies, waits for them, and re-layouts  5.65 us (5%)
    pallas_call x1, Pallas kernels, moment_matrix(): pl.pallas_call(moment_kernel, grid=(blocks,), out_shape=jax.ShapeDtypeStr...  26.6 us
    all_to_all x1, blocking collectives, local(): lax.all_to_all(leaving, axes, split_axis=0, concat_axis=0, tiled=True)  23.4 us
    pallas_call x1, Pallas kernels, project(): pl.pallas_call(project_kernel, grid=(blocks,), out_shape=jax.ShapeDtypeSt...  14.5 us
    pallas_call x1, Pallas kernels, gather(): pl.pallas_call(functools.partial(gather_kernel, subs), grid=(steps,), out...  12.3 us
    all_to_all x1, starting transfers between devices, local(): lax.all_to_all(outgoing, axes, split_axis=0, concat_axis=0, tiled=True)  11.5 us
    all_to_all x1, waiting for transfers between devices, local(): lax.all_to_all(outgoing, axes, split_axis=0, concat_axis=0, tiled=True)  8.24 us
    unnamed x14, local copies, waits for them, and re-layouts  4.32 us
    pallas_call x1, Pallas kernels, index_tables(): pl.pallas_call(index_kernel, out_shape=(jax.ShapeDtypeStruct((slots // LA...  3.59 us
  transfers between devices with their start and end apart: 1, of which 1 were waited for; matrix products, arithmetic and copies ran while one was open for 3% of the time, Pallas kernels for 29%

profile of v5, /device:TPU:1, one launch (start us, length us, event | category | flops | bytes accessed | tf_op | source)
XLA Modules:
  0.0 105.9 jit_solution(9936025889419624964)
XLA Ops:
  0.0 12.3 %gather.1 = f32[6400,128]{1,0:T(8,128)} custom-call(s32[8192]{0:T(1024)} %idx_hbm.1, s32[128,128]{1,0:T(8,128)} %cnt_hbm.1, f32[100,4096]{1,0:T(8,128)} %coef_hbm.1), custom_call_target="tpu_custom_call" | custom-call | tf_op jit(solution)/shard_map/gather/pallas_call | solution.py:89
  12.3 0.0 copy-start
  12.3 0.0 copy-start.1
  12.3 0.0 copy-start.2
  12.3 0.0 copy-start.3
  12.3 11.5 %all-to-all-start = ((f32[128,25,2,128]{3,2,1,0:T(2,128)}), f32[128,25,2,128]{3,2,1,0:T(2,128)S(1)}, u32[]{:S(2)}, u32[]{:S(2)}) async-start(f32[128,25,2,128]{3,2,1,0:T(2,128)} %bitcast.25), calls=%async_computation | async-start | bytes 6553600 | tf_op jit(solution)/shard_map/all_to_all | solution.py:398
  23.9 0.0 copy-done
  23.9 0.0 copy-done.1
  23.9 0.0 copy-done.2
  23.9 0.0 copy-done.3
  23.9 0.0 copy-start.4
  23.9 3.6 %index_tables.1 = (s32[64,128]{1,0:T(8,128)S(1)}, f32[16,128]{1,0:T(8,128)S(1)}, f32[128,112]{1,0:T(8,128)S(1)}) custom-call(s32[2048]{0:T(1024)S(1)} %bitcast.22, s32[64,128]{1,0:T(8,128)S(1)} %bitcast.21, f32[16,128]{1,0:T(8,128)S(1)} %bitcast.24, s32[16,128]{1,0:T(8,128)S(1)} %bitcast.23, f32[20,20]{1,0:T(8,128)S(1)} %copy-done.1), custom_call_target="tpu_custom_call" | custom-call | flops 4400000000 | bytes 8388608 | tf_op jit(solution)/shard_map/index_tables/pallas_call | solution.py:234
  27.5 0.0 copy-start.5
  27.5 0.0 copy-done.4
  27.5 1.6 %copy.13 = f32[1,3,1536,128]{3,2,1,0:T(8,128)} copy(f32[1,3,1536,128]{3,1,2,0:T(4,128)S(1)} %bitcast.27) | data formatting | bytes 4718592
  29.1 1.1 %copy-done.5 = f32[3,196608]{1,0:T(4,128)S(1)} copy-done((f32[3,196608]{1,0:T(4,128)S(1)}, f32[3,196608]{1,0:T(4,128)}, u32[]{:S(2)}) %copy-start.5) | copy-done | bytes 2359320
  30.2 1.6 %copy.14 = f32[1,3,1536,128]{3,2,1,0:T(8,128)} copy(f32[1,3,1536,128]{3,1,2,0:T(4,128)S(1)} %bitcast.28) | data formatting | bytes 4718592
  31.8 26.6 %moment_matrix.1.m_ref = f32[8,400,8,128]{3,2,1,0:T(8,128)} custom-call(f32[3,24,64,128]{3,2,1,0:T(8,128)} %bitcast.29, f32[3,24,64,128]{3,2,1,0:T(8,128)} %bitcast.30, f32[24,64,128]{2,1,0:T(8,128)} %bitcast.31), custom_call_target="tpu_custom_call" | custom-call | flops 22000001024 | bytes 41943040 | tf_op jit(solution)/shard_map/moment_matrix/pallas_call | solution.py:172
  58.5 8.2 %all-to-all-done = f32[128,25,2,128]{3,2,1,0:T(2,128)S(1)} async-done(((f32[128,25,2,128]{3,2,1,0:T(2,128)}), f32[128,25,2,128]{3,2,1,0:T(2,128)S(1)}, u32[]{:S(2)}, u32[]{:S(2)}) %all-to-all-start) | async-done | bytes 3276832 | tf_op jit(solution)/shard_map/all_to_all | solution.py:398
  66.7 14.5 %project.1 = f32[2048,128]{1,0:T(8,128)S(1)} custom-call(f32[6400,128]{1,0:T(8,128)S(1)} %bitcast.18, f32[8,400,8,128]{3,2,1,0:T(8,128)} %moment_matrix.1.m_ref, s32[64,128]{1,0:T(8,128)S(1)} %get-tuple-element.14.target_ref, f32[128,112]{1,0:T(8,128)S(1)} %get-tuple-element.15.minv_ref, f32[1,2048]{1,0:T(1,128)S(1)} %bitcast.20), custom_call_target="tpu_custom_call" | custom-call | tf_op jit(solution)/shard_map/project/pallas_call | solution.py:366
  81.2 23.4 %all_to_all.10 = f32[128,16,128]{2,1,0:T(8,128)S(1)} all-to-all(f32[128,16,128]{2,1,0:T(8,128)S(1)} %bitcast.19), channel_id=1, replica_groups=mesh['dom'=16,'sub'=8] {'dom','sub'}, dimensions={0} | all-to-all | bytes 2097152 | tf_op jit(solution)/shard_map/all_to_all | solution.py:405
  104.6 0.1 slice_bitcast_fusion
  104.7 1.3 %copy.12 = f32[100,2048]{1,0:T(8,128)} copy(f32[100,2048]{0,1:T(8,128)S(1)} %slice_bitcast_fusion) | data formatting | bytes 1638400 | tf_op jit(solution)/shard_map/transpose | solution.py:406
Async XLA Ops:
  12.3 11.6 %copy-start = (s32[8192]{0:T(1024)S(1)}, s32[8192]{0:T(1024)}, u32[]{:S(2)}) copy-start(s32[8192]{0:T(1024)} %param.13) | copy-start | bytes 98308
  12.3 11.6 %copy-start.1 = (f32[20,20]{1,0:T(8,128)S(1)}, f32[20,20]{1,0:T(8,128)}, u32[]{:S(2)}) copy-start(f32[20,20]{1,0:T(8,128)} %minv_ref.1) | copy-start | bytes 4804
  12.3 11.6 %copy-start.2 = (s32[1,2048]{1,0:T(1,128)S(1)}, s32[1,2048]{1,0:T(1,128)}, u32[]{:S(2)}) copy-start(s32[1,2048]{1,0:T(1,128)} %param.19) | copy-start | bytes 24580
  12.3 11.6 %copy-start.3 = (f32[2048]{0:T(1024)S(1)}, f32[2048]{0:T(1024)}, u32[]{:S(2)}) copy-start(f32[2048]{0:T(1024)} %param.17) | copy-start | bytes 24580
  12.3 54.3 %all-to-all-start = ((f32[128,25,2,128]{3,2,1,0:T(2,128)}), f32[128,25,2,128]{3,2,1,0:T(2,128)S(1)}, u32[]{:S(2)}, u32[]{:S(2)}) async-start(f32[128,25,2,128]{3,2,1,0:T(2,128)} %bitcast.25), calls=%async_computation | async-start | bytes 6553600 | tf_op jit(solution)/shard_map/all_to_all | solution.py:398
  23.9 3.6 %copy-start.4 = (f32[3,196608]{1,0:T(4,128)S(1)}, f32[3,196608]{1,0:T(4,128)}, u32[]{:S(2)}) copy-start(f32[3,196608]{1,0:T(4,128)} %param.14) | copy-start | bytes 7077892
  27.5 2.7 %copy-start.5 = (f32[3,196608]{1,0:T(4,128)S(1)}, f32[3,196608]{1,0:T(4,128)}, u32[]{:S(2)}) copy-start(f32[3,196608]{1,0:T(4,128)} %param.15) | copy-start | bytes 7077892

commit v6 on v5

--- a/solution.py
+++ b/solution.py
@@ -255,11 +255,14 @@
 
 
 PADH = 56
+SHARE = 16
+TALL = 13
+CUT = 25
 BINS = 512
 
 
 def project_kernel(
-    recv_ref, m_ref, target_ref, minv_ref, jac_ref, out_ref, coef_ref, y0, y1, lhs0, lhs1, acc0, acc1
+    recv_ref, m_ref, target_ref, minv_ref, jac_ref, out_ref, coef_ref, y0, y1, lhs0, lhs1, acc0, acc1, turned_ref
 ):
     turn = pl.program_id(0)
     folds = acc0.shape[0] // (2 * PADH)
@@ -288,7 +291,7 @@
         wanted = (within - 256 * h).astype(single).astype(half)
         parts.append(jnp.where(bins == wanted, jnp.array(1, half), jnp.array(0, half)))
     hot = jnp.concatenate(parts, axis=0)
-    tile = 5
+    tile = 2
     span = MODES // 2
 
     def apply(y_ref, start):
@@ -354,9 +357,23 @@
             done = jnp.dot(left, right, preferred_element_type=single)
             done = done * scale[:, a * BINS : (a + 1) * BINS]
             for j in range(BINS // LANES):
-                out_ref[a * BINS + j * LANES : a * BINS + (j + 1) * LANES, :] = done[
+                turned_ref[a * BINS + j * LANES : a * BINS + (j + 1) * LANES, :] = done[
                     :, j * LANES : (j + 1) * LANES
                 ].T
+        lane = lax.broadcasted_iota(jnp.int32, (8, LANES), 1)
+        for g in range(turned_ref.shape[0] // LANES):
+            for i in range(SHARE - TALL):
+                extra = turned_ref[pl.ds(g * LANES + TALL + i, 8, stride=SHARE), :]
+                for c in range(4):
+                    r = 4 * i + c
+                    kept = turned_ref[pl.ds(g * LANES + r, 8, stride=SHARE), :]
+                    moved = pltpu.roll(extra, ROWS - CUT * c, 1)
+                    out_ref[pl.ds(g * 8 * TALL + r, 8, stride=TALL), :] = jnp.where(
+                        lane < ROWS, kept, moved
+                    )
+            out_ref[pl.ds(g * 8 * TALL + TALL - 1, 8, stride=TALL), :] = turned_ref[
+                pl.ds(g * LANES + TALL - 1, 8, stride=SHARE), :
+            ]
 
 
 def project(received, matrix, target, minv, jac):
@@ -366,7 +383,7 @@
     return pl.pallas_call(
         project_kernel,
         grid=(blocks,),
-        out_shape=jax.ShapeDtypeStruct((count, LANES), jnp.float32),
+        out_shape=jax.ShapeDtypeStruct((count // SHARE * TALL, LANES), jnp.float32),
         in_specs=[
             pl.BlockSpec(memory_space=pltpu.VMEM),
             pl.BlockSpec((1, MODES * MODES, 8, LANES), lambda i: (i, 0, 0, 0)),
@@ -374,7 +391,7 @@
             pl.BlockSpec((LANES, 2 * PADH), lambda i: (0, 0)),
             pl.BlockSpec((1, count), lambda i: (0, 0)),
         ],
-        out_specs=pl.BlockSpec((count, LANES), lambda i: (0, 0)),
+        out_specs=pl.BlockSpec((count // SHARE * TALL, LANES), lambda i: (0, 0)),
         scratch_shapes=[
             pltpu.VMEM((ROWS, 8, LANES), jnp.float32),
             pltpu.VMEM((PADH * 8, LANES), jnp.float32),
@@ -383,10 +400,44 @@
             pltpu.VMEM((folds * 2 * PADH, 8 * LANES), jnp.bfloat16),
             pltpu.VMEM((folds * 2 * PADH, BINS), jnp.float32),
             pltpu.VMEM((folds * 2 * PADH, BINS), jnp.float32),
+            pltpu.VMEM((count, LANES), jnp.float32),
         ],
         compiler_params=pltpu.CompilerParams(vmem_limit_bytes=44 << 20),
         name="project",
     )(received, matrix, target, minv, jac)
+
+
+def arrange_kernel(in_ref, out_ref, turned_ref):
+    lane = lax.broadcasted_iota(jnp.int32, (8, LANES), 1)
+    for g in range(out_ref.shape[1] // LANES):
+        for i in range(SHARE - TALL):
+            extra = jnp.zeros((8, LANES), jnp.float32)
+            for c in range(4):
+                r = 4 * i + c
+                row = in_ref[pl.ds(g * 8 * TALL + r, 8, stride=TALL), :]
+                turned_ref[pl.ds(g * LANES + r, 8, stride=SHARE), :] = row
+                moved = pltpu.roll(row, LANES - ROWS + CUT * c, 1)
+                extra = jnp.where((lane >= CUT * c) & (lane < CUT * (c + 1)), moved, extra)
+            turned_ref[pl.ds(g * LANES + TALL + i, 8, stride=SHARE), :] = extra
+        turned_ref[pl.ds(g * LANES + TALL - 1, 8, stride=SHARE), :] = in_ref[
+            pl.ds(g * 8 * TALL + TALL - 1, 8, stride=TALL), :
+        ]
+    for g in range(out_ref.shape[1] // LANES):
+        span = slice(g * LANES, (g + 1) * LANES)
+        out_ref[:, span] = turned_ref[span, :].T[:ROWS]
+
+
+def arrange(arrived):
+    width = arrived.shape[0] // TALL * SHARE
+    return pl.pallas_call(
+        arrange_kernel,
+        out_shape=jax.ShapeDtypeStruct((ROWS, width), jnp.float32),
+        in_specs=[pl.BlockSpec(memory_space=pltpu.VMEM)],
+        out_specs=pl.BlockSpec(memory_space=pltpu.VMEM),
+        scratch_shapes=[pltpu.VMEM((width, LANES), jnp.float32)],
+        compiler_params=pltpu.CompilerParams(vmem_limit_bytes=24 << 20),
+        name="arrange",
+    )(arrived)
 
 
 def local(old_coef, old_index, pair_count, new_index, old_points, new_points, weights, jacobian,
@@ -401,9 +452,9 @@
     old_points, new_points, target = lax.optimization_barrier((old_points, new_points, target))
     matrix = moment_matrix(old_points, new_points, weights)
     leaving = project(received, matrix, target, minv, jac.reshape(1, -1))
-    leaving = leaving.reshape(devices, -1, LANES)
+    leaving = leaving.reshape(devices, TALL, 1, LANES)
     arrived = lax.all_to_all(leaving, axes, split_axis=0, concat_axis=0, tiled=True)
-    return arrived.reshape(-1, LANES)[:, :ROWS].T
+    return arrange(arrived.reshape(-1, LANES))
 
 
 def solution(mesh):

time: 106 us -> 105 us (level)
  blocking collectives: 23.4 us -> 21.3 us
  Pallas kernels: 57.1 us -> 58.7 us
  local copies, waits for them, and re-layouts: 5.65 us -> 4.32 us
    all_to_all x1, blocking collectives: 23.4 us -> 21.3 us  [local(): lax.all_to_all(leaving, axes, split_axis=0, concat_axis=0, tiled=True)]
    pallas_call x0 -> x1, Pallas kernels: none -> 1.6 us  [arrange(): pl.pallas_call(arrange_kernel, out_shape=jax.ShapeDtypeStruct((ROWS, widt...]
    transpose x2 -> x0, local copies, waits for them, and re-layouts: 1.34 us -> none  [local(): return arrived.reshape(-1, LANES)[:, :ROWS].T]
where the time goes in v6:
time: 105 us; the launch traced here: 104 us
  Pallas kernels  58.7 us (56%)
  blocking collectives  21.3 us (20%)
  starting transfers between devices  11.5 us (11%)
  waiting for transfers between devices  8.24 us (8%)
  local copies, waits for them, and re-layouts  4.32 us (4%)
    pallas_call x1, Pallas kernels, moment_matrix(): pl.pallas_call(moment_kernel, grid=(blocks,), out_shape=jax.ShapeDtypeStr...  26.6 us
    all_to_all x1, blocking collectives, local(): lax.all_to_all(leaving, axes, split_axis=0, concat_axis=0, tiled=True)  21.3 us
    pallas_call x1, Pallas kernels, project(): pl.pallas_call(project_kernel, grid=(blocks,), out_shape=jax.ShapeDtypeSt...  14.6 us
    pallas_call x1, Pallas kernels, gather(): pl.pallas_call(functools.partial(gather_kernel, subs), grid=(steps,), out...  12.3 us
    all_to_all x1, starting transfers between devices, local(): lax.all_to_all(outgoing, axes, split_axis=0, concat_axis=0, tiled=True)  11.5 us
    all_to_all x1, waiting for transfers between devices, local(): lax.all_to_all(outgoing, axes, split_axis=0, concat_axis=0, tiled=True)  8.24 us
    unnamed x14, local copies, waits for them, and re-layouts  4.32 us
    pallas_call x1, Pallas kernels, index_tables(): pl.pallas_call(index_kernel, out_shape=(jax.ShapeDtypeStruct((slots // LA...  3.59 us
  transfers between devices with their start and end apart: 1, of which 1 were waited for; matrix products, arithmetic and copies ran while one was open for 3% of the time, Pallas kernels for 29%

profile of v6, /device:TPU:1, one launch (start us, length us, event | category | flops | bytes accessed | tf_op | source)
XLA Modules:
  0.0 104.2 jit_solution(8451524552941728222)
XLA Ops:
  0.0 12.3 %gather.1 = f32[6400,128]{1,0:T(8,128)} custom-call(s32[8192]{0:T(1024)} %idx_hbm.1, s32[128,128]{1,0:T(8,128)} %cnt_hbm.1, f32[100,4096]{1,0:T(8,128)} %coef_hbm.1), custom_call_target="tpu_custom_call" | custom-call | tf_op jit(solution)/shard_map/gather/pallas_call | solution.py:89
  12.3 0.0 copy-start
  12.3 0.0 copy-start.1
  12.3 0.0 copy-start.2
  12.3 0.0 copy-start.3
  12.3 11.5 %all-to-all-start = ((f32[128,25,2,128]{3,2,1,0:T(2,128)}), f32[128,25,2,128]{3,2,1,0:T(2,128)S(1)}, u32[]{:S(2)}, u32[]{:S(2)}) async-start(f32[128,25,2,128]{3,2,1,0:T(2,128)} %bitcast.24), calls=%async_computation | async-start | bytes 6553600 | tf_op jit(solution)/shard_map/all_to_all | solution.py:449
  23.9 0.0 copy-done
  23.9 0.0 copy-done.1
  23.9 0.0 copy-done.2
  23.9 0.0 copy-done.3
  23.9 0.0 copy-start.4
  23.9 3.6 %index_tables.1 = (s32[64,128]{1,0:T(8,128)S(1)}, f32[16,128]{1,0:T(8,128)S(1)}, f32[128,112]{1,0:T(8,128)S(1)}) custom-call(s32[2048]{0:T(1024)S(1)} %bitcast.21, s32[64,128]{1,0:T(8,128)S(1)} %bitcast.20, f32[16,128]{1,0:T(8,128)S(1)} %bitcast.23, s32[16,128]{1,0:T(8,128)S(1)} %bitcast.22, f32[20,20]{1,0:T(8,128)S(1)} %copy-done.1), custom_call_target="tpu_custom_call" | custom-call | flops 4400000000 | bytes 8388608 | tf_op jit(solution)/shard_map/index_tables/pallas_call | solution.py:234
  27.5 0.0 copy-start.5
  27.5 0.0 copy-done.4
  27.5 1.6 %copy.12 = f32[1,3,1536,128]{3,2,1,0:T(8,128)} copy(f32[1,3,1536,128]{3,1,2,0:T(4,128)S(1)} %bitcast.25) | data formatting | bytes 4718592
  29.1 1.1 %copy-done.5 = f32[3,196608]{1,0:T(4,128)S(1)} copy-done((f32[3,196608]{1,0:T(4,128)S(1)}, f32[3,196608]{1,0:T(4,128)}, u32[]{:S(2)}) %copy-start.5) | copy-done | bytes 2359320
  30.2 1.6 %copy.13 = f32[1,3,1536,128]{3,2,1,0:T(8,128)} copy(f32[1,3,1536,128]{3,1,2,0:T(4,128)S(1)} %bitcast.26) | data formatting | bytes 4718592
  31.8 26.6 %moment_matrix.1.m_ref = f32[8,400,8,128]{3,2,1,0:T(8,128)} custom-call(f32[3,24,64,128]{3,2,1,0:T(8,128)} %bitcast.27, f32[3,24,64,128]{3,2,1,0:T(8,128)} %bitcast.28, f32[24,64,128]{2,1,0:T(8,128)} %bitcast.29), custom_call_target="tpu_custom_call" | custom-call | flops 22000001024 | bytes 41943040 | tf_op jit(solution)/shard_map/moment_matrix/pallas_call | solution.py:172
  58.5 8.2 %all-to-all-done = f32[128,25,2,128]{3,2,1,0:T(2,128)S(1)} async-done(((f32[128,25,2,128]{3,2,1,0:T(2,128)}), f32[128,25,2,128]{3,2,1,0:T(2,128)S(1)}, u32[]{:S(2)}, u32[]{:S(2)}) %all-to-all-start) | async-done | bytes 3276832 | tf_op jit(solution)/shard_map/all_to_all | solution.py:449
  66.7 14.6 %project.1 = f32[1664,128]{1,0:T(8,128)S(1)} custom-call(f32[6400,128]{1,0:T(8,128)S(1)} %bitcast.16, f32[8,400,8,128]{3,2,1,0:T(8,128)} %moment_matrix.1.m_ref, s32[64,128]{1,0:T(8,128)S(1)} %get-tuple-element.14.target_ref, f32[128,112]{1,0:T(8,128)S(1)} %get-tuple-element.15.minv_ref, f32[1,2048]{1,0:T(1,128)S(1)} %bitcast.19), custom_call_target="tpu_custom_call" | custom-call | tf_op jit(solution)/shard_map/project/pallas_call | solution.py:383
  81.3 21.3 %all_to_all.10 = f32[128,13,1,128]{3,2,1,0:T(1,128)S(1)} all-to-all(f32[128,13,1,128]{3,2,1,0:T(1,128)S(1)} %bitcast.18), channel_id=1, replica_groups=mesh['dom'=16,'sub'=8] {'dom','sub'}, dimensions={0} | all-to-all | bytes 1703936 | tf_op jit(solution)/shard_map/all_to_all | solution.py:456
  102.6 1.6 %arrange.1 = f32[100,2048]{1,0:T(8,128)} custom-call(f32[1664,128]{1,0:T(8,128)S(1)} %bitcast.17), custom_call_target="tpu_custom_call" | custom-call | tf_op jit(solution)/shard_map/arrange/pallas_call | solution.py:432
Async XLA Ops:
  12.3 11.6 %copy-start = (s32[8192]{0:T(1024)S(1)}, s32[8192]{0:T(1024)}, u32[]{:S(2)}) copy-start(s32[8192]{0:T(1024)} %param.13) | copy-start | bytes 98308
  12.3 11.6 %copy-start.1 = (f32[20,20]{1,0:T(8,128)S(1)}, f32[20,20]{1,0:T(8,128)}, u32[]{:S(2)}) copy-start(f32[20,20]{1,0:T(8,128)} %minv_ref.1) | copy-start | bytes 4804
  12.3 11.6 %copy-start.2 = (s32[1,2048]{1,0:T(1,128)S(1)}, s32[1,2048]{1,0:T(1,128)}, u32[]{:S(2)}) copy-start(s32[1,2048]{1,0:T(1,128)} %param.19) | copy-start | bytes 24580
  12.3 11.6 %copy-start.3 = (f32[2048]{0:T(1024)S(1)}, f32[2048]{0:T(1024)}, u32[]{:S(2)}) copy-start(f32[2048]{0:T(1024)} %param.17) | copy-start | bytes 24580
  12.3 54.3 %all-to-all-start = ((f32[128,25,2,128]{3,2,1,0:T(2,128)}), f32[128,25,2,128]{3,2,1,0:T(2,128)S(1)}, u32[]{:S(2)}, u32[]{:S(2)}) async-start(f32[128,25,2,128]{3,2,1,0:T(2,128)} %bitcast.24), calls=%async_computation | async-start | bytes 6553600 | tf_op jit(solution)/shard_map/all_to_all | solution.py:449
  23.9 3.6 %copy-start.4 = (f32[3,196608]{1,0:T(4,128)S(1)}, f32[3,196608]{1,0:T(4,128)}, u32[]{:S(2)}) copy-start(f32[3,196608]{1,0:T(4,128)} %param.14) | copy-start | bytes 7077892
  27.5 2.7 %copy-start.5 = (f32[3,196608]{1,0:T(4,128)S(1)}, f32[3,196608]{1,0:T(4,128)}, u32[]{:S(2)}) copy-start(f32[3,196608]{1,0:T(4,128)} %param.15) | copy-start | bytes 7077892

commit v7 on v6

--- a/solution.py
+++ b/solution.py
@@ -63,8 +63,19 @@
     def fetch(t, carry):
         base = pl.multiple_of(t * LANES, LANES)
         first = (part * pairs + t) * LANES
-        for j in range(LANES):
-            buf_ref[pl.ds(base + j, 1), :] = tab_ref[pl.ds(idx_ref[first + j], 1), :]
+        def take(begin, end):
+            for j in range(begin, end):
+                buf_ref[pl.ds(base + j, 1), :] = tab_ref[pl.ds(idx_ref[first + j], 1), :]
+
+        for side in range(2):
+            used = cnt_ref[myself, 2 * (part * pairs + t) + side]
+            for begin, end in ((0, 40), (40, 64)):
+                if begin == 0:
+                    take(side * CAP, side * CAP + end)
+                else:
+                    pl.when(used > begin)(
+                        functools.partial(take, side * CAP + begin, side * CAP + end)
+                    )
         return carry
 
     lax.fori_loop(0, pairs, fetch, 0)

time: 105 us -> 104 us (level)
  no operation moved by 1% of the time
where the time goes in v7:
time: 104 us
  Pallas kernels  58.4 us (56%)
  blocking collectives  21.3 us (20%)
  starting transfers between devices  11.5 us (11%)
  waiting for transfers between devices  8.24 us (8%)
  local copies, waits for them, and re-layouts  4.32 us (4%)
    pallas_call x1, Pallas kernels, moment_matrix(): pl.pallas_call(moment_kernel, grid=(blocks,), out_shape=jax.ShapeDtypeStr...  26.6 us
    all_to_all x1, blocking collectives, local(): lax.all_to_all(leaving, axes, split_axis=0, concat_axis=0, tiled=True)  21.3 us
    pallas_call x1, Pallas kernels, project(): pl.pallas_call(project_kernel, grid=(blocks,), out_shape=jax.ShapeDtypeSt...  14.6 us
    pallas_call x1, Pallas kernels, gather(): pl.pallas_call(functools.partial(gather_kernel, subs), grid=(steps,), out...  12 us
    all_to_all x1, starting transfers between devices, local(): lax.all_to_all(outgoing, axes, split_axis=0, concat_axis=0, tiled=True)  11.5 us
    all_to_all x1, waiting for transfers between devices, local(): lax.all_to_all(outgoing, axes, split_axis=0, concat_axis=0, tiled=True)  8.24 us
    unnamed x14, local copies, waits for them, and re-layouts  4.32 us
    pallas_call x1, Pallas kernels, index_tables(): pl.pallas_call(index_kernel, out_shape=(jax.ShapeDtypeStruct((slots // LA...  3.59 us
  transfers between devices with their start and end apart: 1, of which 1 were waited for; matrix products, arithmetic and copies ran while one was open for 3% of the time, Pallas kernels for 29%

profile of v7, /device:TPU:1, one launch (start us, length us, event | category | flops | bytes accessed | tf_op | source)
XLA Modules:
  0.0 103.8 jit_solution(3552433916582810049)
XLA Ops:
  0.0 12.0 %gather.1 = f32[6400,128]{1,0:T(8,128)} custom-call(s32[8192]{0:T(1024)} %idx_hbm.1, s32[128,128]{1,0:T(8,128)} %cnt_hbm.1, f32[100,4096]{1,0:T(8,128)} %coef_hbm.1), custom_call_target="tpu_custom_call" | custom-call | tf_op jit(solution)/shard_map/gather/pallas_call | solution.py:100
  12.0 0.0 copy-start
  12.0 0.0 copy-start.1
  12.0 0.0 copy-start.2
  12.0 0.0 copy-start.3
  12.0 11.5 %all-to-all-start = ((f32[128,25,2,128]{3,2,1,0:T(2,128)}), f32[128,25,2,128]{3,2,1,0:T(2,128)S(1)}, u32[]{:S(2)}, u32[]{:S(2)}) async-start(f32[128,25,2,128]{3,2,1,0:T(2,128)} %bitcast.24), calls=%async_computation | async-start | bytes 6553600 | tf_op jit(solution)/shard_map/all_to_all | solution.py:460
  23.5 0.0 copy-done
  23.5 0.0 copy-done.1
  23.5 0.0 copy-done.2
  23.5 0.0 copy-done.3
  23.5 0.0 copy-start.4
  23.6 3.6 %index_tables.1 = (s32[64,128]{1,0:T(8,128)S(1)}, f32[16,128]{1,0:T(8,128)S(1)}, f32[128,112]{1,0:T(8,128)S(1)}) custom-call(s32[2048]{0:T(1024)S(1)} %bitcast.21, s32[64,128]{1,0:T(8,128)S(1)} %bitcast.20, f32[16,128]{1,0:T(8,128)S(1)} %bitcast.23, s32[16,128]{1,0:T(8,128)S(1)} %bitcast.22, f32[20,20]{1,0:T(8,128)S(1)} %copy-done.1), custom_call_target="tpu_custom_call" | custom-call | flops 4400000000 | bytes 8388608 | tf_op jit(solution)/shard_map/index_tables/pallas_call | solution.py:245
  27.2 0.0 copy-start.5
  27.2 0.0 copy-done.4
  27.2 1.6 %copy.12 = f32[1,3,1536,128]{3,2,1,0:T(8,128)} copy(f32[1,3,1536,128]{3,1,2,0:T(4,128)S(1)} %bitcast.25) | data formatting | bytes 4718592
  28.8 1.1 %copy-done.5 = f32[3,196608]{1,0:T(4,128)S(1)} copy-done((f32[3,196608]{1,0:T(4,128)S(1)}, f32[3,196608]{1,0:T(4,128)}, u32[]{:S(2)}) %copy-start.5) | copy-done | bytes 2359320
  29.9 1.6 %copy.13 = f32[1,3,1536,128]{3,2,1,0:T(8,128)} copy(f32[1,3,1536,128]{3,1,2,0:T(4,128)S(1)} %bitcast.26) | data formatting | bytes 4718592
  31.5 26.6 %moment_matrix.1.m_ref = f32[8,400,8,128]{3,2,1,0:T(8,128)} custom-call(f32[3,24,64,128]{3,2,1,0:T(8,128)} %bitcast.27, f32[3,24,64,128]{3,2,1,0:T(8,128)} %bitcast.28, f32[24,64,128]{2,1,0:T(8,128)} %bitcast.29), custom_call_target="tpu_custom_call" | custom-call | flops 22000001024 | bytes 41943040 | tf_op jit(solution)/shard_map/moment_matrix/pallas_call | solution.py:183
  58.1 8.2 %all-to-all-done = f32[128,25,2,128]{3,2,1,0:T(2,128)S(1)} async-done(((f32[128,25,2,128]{3,2,1,0:T(2,128)}), f32[128,25,2,128]{3,2,1,0:T(2,128)S(1)}, u32[]{:S(2)}, u32[]{:S(2)}) %all-to-all-start) | async-done | bytes 3276832 | tf_op jit(solution)/shard_map/all_to_all | solution.py:460
  66.3 14.6 %project.1 = f32[1664,128]{1,0:T(8,128)S(1)} custom-call(f32[6400,128]{1,0:T(8,128)S(1)} %bitcast.16, f32[8,400,8,128]{3,2,1,0:T(8,128)} %moment_matrix.1.m_ref, s32[64,128]{1,0:T(8,128)S(1)} %get-tuple-element.14.target_ref, f32[128,112]{1,0:T(8,128)S(1)} %get-tuple-element.15.minv_ref, f32[1,2048]{1,0:T(1,128)S(1)} %bitcast.19), custom_call_target="tpu_custom_call" | custom-call | tf_op jit(solution)/shard_map/project/pallas_call | solution.py:394
  81.0 21.3 %all_to_all.10 = f32[128,13,1,128]{3,2,1,0:T(1,128)S(1)} all-to-all(f32[128,13,1,128]{3,2,1,0:T(1,128)S(1)} %bitcast.18), channel_id=1, replica_groups=mesh['dom'=16,'sub'=8] {'dom','sub'}, dimensions={0} | all-to-all | bytes 1703936 | tf_op jit(solution)/shard_map/all_to_all | solution.py:467
  102.2 1.6 %arrange.1 = f32[100,2048]{1,0:T(8,128)} custom-call(f32[1664,128]{1,0:T(8,128)S(1)} %bitcast.17), custom_call_target="tpu_custom_call" | custom-call | tf_op jit(solution)/shard_map/arrange/pallas_call | solution.py:443
Async XLA Ops:
  12.0 11.5 %copy-start = (s32[8192]{0:T(1024)S(1)}, s32[8192]{0:T(1024)}, u32[]{:S(2)}) copy-start(s32[8192]{0:T(1024)} %param.13) | copy-start | bytes 98308
  12.0 11.5 %copy-start.1 = (f32[20,20]{1,0:T(8,128)S(1)}, f32[20,20]{1,0:T(8,128)}, u32[]{:S(2)}) copy-start(f32[20,20]{1,0:T(8,128)} %minv_ref.1) | copy-start | bytes 4804
  12.0 11.5 %copy-start.2 = (s32[1,2048]{1,0:T(1,128)S(1)}, s32[1,2048]{1,0:T(1,128)}, u32[]{:S(2)}) copy-start(s32[1,2048]{1,0:T(1,128)} %param.19) | copy-start | bytes 24580
  12.0 11.5 %copy-start.3 = (f32[2048]{0:T(1024)S(1)}, f32[2048]{0:T(1024)}, u32[]{:S(2)}) copy-start(f32[2048]{0:T(1024)} %param.17) | copy-start | bytes 24580
  12.0 54.3 %all-to-all-start = ((f32[128,25,2,128]{3,2,1,0:T(2,128)}), f32[128,25,2,128]{3,2,1,0:T(2,128)S(1)}, u32[]{:S(2)}, u32[]{:S(2)}) async-start(f32[128,25,2,128]{3,2,1,0:T(2,128)} %bitcast.24), calls=%async_computation | async-start | bytes 6553600 | tf_op jit(solution)/shard_map/all_to_all | solution.py:460
  23.5 3.6 %copy-start.4 = (f32[3,196608]{1,0:T(4,128)S(1)}, f32[3,196608]{1,0:T(4,128)}, u32[]{:S(2)}) copy-start(f32[3,196608]{1,0:T(4,128)} %param.14) | copy-start | bytes 7077892
  27.2 2.7 %copy-start.5 = (f32[3,196608]{1,0:T(4,128)S(1)}, f32[3,196608]{1,0:T(4,128)}, u32[]{:S(2)}) copy-start(f32[3,196608]{1,0:T(4,128)} %param.15) | copy-start | bytes 7077892
